TPU v7x, 32 devices: a whole 2x2x4 slice. The times are simulated.
32 devices in a mesh: grp: 2 (over y), chan: 4 (over z), sub: 4 (over x, core).
Axes of the slice: x: 2, y: 2, z: 4, core: 2. Of those that a mesh axis runs over, the one named last changes fastest.
Arguments:
- voltages: bfloat16 [2048, 2, 5504], P(('grp', 'chan', 'sub')), parts along dimension 0, may hold values from -6 to 6
- taps: float32 [1536], replicated, may hold values from -0.15625 to 0.15625
- input_id: int32 [1024], replicated, may hold values from 0 to 1023, each once
- counts: int32 [8], P('grp'), parts along dimension 0, may hold values from 2 to 8, as said below
- delays: int32 [512, 1024], P(('grp', 'sub')), parts along dimension 0, may hold values from 0 to 127
- beam_owner: int32 [512, 1], P('grp'), parts along dimension 0, may hold values from 0 to 3; in each aligned block of 64 rows (0 to 63, 64 to 127, ...) at most 32 rows name the same one
Outputs:
- visibility: bfloat16 [256, 2, 1024, 1024], P(('grp', 'chan'), None, 'sub'), parts along dimension 0
- resynth: float32 [1024, 2, 5504], P(('grp', 'chan', 'sub')), parts along dimension 0
There are 2 independent parts, one for each index of `grp`. A program takes and returns all parts, laid end to end along the dimension named above; an argument that names none is the same for every part. Nothing has to cross between parts.
Inputs may be any that keep to these rules, and one draw needn't show every extreme that they name: `input_id`: each input id appears once. `counts`: every draw has a block with all 8 spectra valid. `beam_owner`: within each section of 64 consecutive beams no owner is named more than 32 times; some owner is named exactly 32 times in some section.
All inputs are finite; a program needn't handle non-finite values.
Results may differ from a plain program's by a relative error of at most 0.007.
Values may be sent and summed in bfloat16 or wider, within the bound.
A program may use at most 192 MiB of HBM per device.

v0:
```python
import math

import jax
import jax.numpy as jnp
from jax import lax
from jax.sharding import PartitionSpec as P

NCH = 128
TAPS = 12
SPEC = 8
BLOCKS = 4
BEAMS = 256


def filter_table(taps, chans):
    length = taps.shape[0]
    position = jnp.arange(length, dtype=jnp.int32) % chans
    channel = jnp.arange(chans, dtype=jnp.int32)
    phase = (position[:, None] * channel[None, :] % chans).astype(jnp.float32) * (
        2.0 * math.pi / chans
    )
    cosine = taps[:, None] * jnp.cos(phase)
    sine = taps[:, None] * jnp.sin(phase)
    upper = jnp.concatenate([cosine, -sine], axis=1)
    lower = jnp.concatenate([sine, cosine], axis=1)
    return jnp.concatenate([upper, lower], axis=0).astype(jnp.bfloat16)


def resynthesize(received, table, taps_count, chans):
    count = received.shape[0]
    spectra_n = received.shape[3]
    table3 = table.reshape(2 * taps_count * chans, 2, chans)
    grid = jnp.einsum("pcht,mch->ptm", received, table3, preferred_element_type=jnp.float32)
    grid = grid.reshape(count, spectra_n, 2, taps_count, chans)
    total = jnp.zeros((count, spectra_n + taps_count - 1, 2, chans), jnp.float32)
    for k in range(taps_count):
        total = total + jnp.pad(
            grid[:, :, :, k, :], ((0, 0), (k, taps_count - 1 - k), (0, 0), (0, 0))
        )
    return jnp.transpose(total, (0, 2, 1, 3)).reshape(
        count, 2, (spectra_n + taps_count - 1) * chans
    )


def local(voltages, taps, input_id, counts, delays, beam_owner):
    n_chan = lax.axis_size("chan")
    n_sub = lax.axis_size("sub")
    inp_dev = voltages.shape[0]
    inputs = input_id.shape[0]
    chans = NCH
    taps_count = TAPS
    spectra_n = BLOCKS * SPEC
    ch_dev = chans // n_chan
    rows = inputs // n_sub
    section = BEAMS // n_sub
    most = min(section, max(2, 2 * section // n_chan))
    table = filter_table(taps, chans)
    position = jnp.arange(spectra_n, dtype=jnp.int32)
    valid = (position % SPEC < jnp.repeat(counts, SPEC)).astype(jnp.float32)
    total = jnp.sum(counts.astype(jnp.float32))
    frames = voltages.reshape(inp_dev, 2, spectra_n + taps_count - 1, chans)
    windows = jnp.concatenate(
        [frames[:, :, k : k + spectra_n, :] for k in range(taps_count)], axis=3
    )
    table3 = table.reshape(2, taps_count * chans, 2 * chans)
    filtered = jnp.einsum("icth,chm->mit", windows, table3, preferred_element_type=jnp.float32)
    filtered = filtered * valid[None, None, :]
    spectra = filtered.reshape(2, chans, inp_dev, spectra_n).astype(jnp.bfloat16)
    slot_of = jnp.zeros((inputs,), jnp.int32).at[input_id].set(jnp.arange(inputs, dtype=jnp.int32))
    turned = lax.all_to_all(spectra, "chan", split_axis=1, concat_axis=2, tiled=True)
    gathered = lax.all_gather(turned, "sub", axis=2, tiled=True)
    chan_part = slot_of // (n_sub * inp_dev)
    sub_part = slot_of // inp_dev % n_sub
    order = (sub_part * n_chan + chan_part) * inp_dev + slot_of % inp_dev
    by_id = jnp.take(gathered, order, axis=2)
    sub_index = lax.axis_index("sub")
    mine = lax.dynamic_slice_in_dim(by_id, sub_index * rows, rows, 2)
    real_part = jnp.einsum("cxit,cxjt->xij", mine, by_id, preferred_element_type=jnp.float32)
    imag_part = jnp.einsum("xit,xjt->xij", mine[1], by_id[0], preferred_element_type=jnp.float32)
    imag_part = imag_part - jnp.einsum(
        "xit,xjt->xij", mine[0], by_id[1], preferred_element_type=jnp.float32
    )
    visibility = (jnp.stack([real_part, imag_part], axis=1) / total).astype(jnp.bfloat16)
    channel = lax.axis_index("chan") * ch_dev + jnp.arange(ch_dev, dtype=jnp.int32)
    phase = (delays[None, :, :] * channel[:, None, None] % chans).astype(jnp.float32) * (
        2.0 * math.pi / chans
    )
    scale = 1.0 / math.sqrt(inputs)
    weight_cos = (jnp.cos(phase) * scale).astype(jnp.bfloat16)
    weight_sin = (jnp.sin(phase) * scale).astype(jnp.bfloat16)
    from_cos = jnp.einsum("xbi,cxit->cxbt", weight_cos, by_id, preferred_element_type=jnp.float32)
    from_sin = jnp.einsum("xbi,cxit->cxbt", weight_sin, by_id, preferred_element_type=jnp.float32)
    beams = jnp.stack([from_cos[0] - from_sin[1], from_cos[1] + from_sin[0]]).astype(jnp.bfloat16)
    owner = lax.dynamic_slice_in_dim(beam_owner[:, 0], sub_index * section, section)
    beam = jnp.arange(section, dtype=jnp.int32)
    earlier = (owner[None, :] == owner[:, None]) & (beam[None, :] < beam[:, None])
    rank = jnp.sum(earlier.astype(jnp.int32), axis=1)
    target = owner * most + rank
    select = (jnp.arange(n_chan * most, dtype=jnp.int32)[:, None] == target[None, :]).astype(
        jnp.bfloat16
    )
    placed = jnp.einsum("pb,cxbt->pcxt", select, beams, preferred_element_type=jnp.float32).astype(
        jnp.bfloat16
    )
    placed = placed.reshape(n_chan, most, 2, ch_dev, spectra_n)
    resynth = resynthesize(
        lax.all_to_all(placed, "chan", split_axis=0, concat_axis=3, tiled=True)[0],
        table,
        taps_count,
        chans,
    )
    return (visibility, resynth)


def solution(mesh):
    placed = (
        P(("grp", "chan", "sub"), None, None),
        P(),
        P(),
        P("grp"),
        P(("grp", "sub"), None),
        P("grp", None),
    )
    return jax.shard_map(
        local,
        mesh=mesh,
        in_specs=placed,
        out_specs=(P(("grp", "chan"), None, "sub", None), P(("grp", "chan", "sub"), None, None)),
        check_vma=False,
    )
```

profile of v0, /device:TPU:0, one launch (start us, length us, event | category | flops | bytes accessed | tf_op | source)
XLA Modules:
  0.0 463.8 jit_solution(4813590015660750824)
XLA Ops:
  8.0 3.7 reshape.232
  11.7 3.5 fusion.74
  16.0 4.4 negate_convert_fusion.1
  20.4 0.9 copy_dynamic-update-slice_fusion.10
  21.2 0.9 copy_dynamic-update-slice_fusion.9
  22.1 0.9 copy_dynamic-update-slice_fusion.8
  22.9 0.9 copy_dynamic-update-slice_fusion.7
  23.8 0.9 copy_dynamic-update-slice_fusion.6
  24.7 0.9 copy_dynamic-update-slice_fusion.5
  25.5 0.9 copy_dynamic-update-slice_fusion.4
  26.4 0.9 copy_dynamic-update-slice_fusion.3
  27.3 0.9 copy_dynamic-update-slice_fusion.2
  28.1 0.9 copy_dynamic-update-slice_fusion.1
  29.9 4.8 %copy-done.3 = bf16[64,2,32,1536]{3,0,1,2:T(8,128)(2,1)} copy-done((bf16[64,2,32,1536]{3,0,1,2:T(8,128)(2,1)}, bf16[64,2,32,1536]{3,0,1,2:T(8,128)(2,1)S(1)}, u32[]{:S(2)}) %copy-start.3) | copy-done | bytes 12582936
  34.8 8.5 %fusion.15 = bf16[256,64,32]{0,1,2:T(8,128)(2,1)S(1)} fusion(bf16[2,1536,256,1]{2,1,0,3:T(8,128)(2,1)S(1)} %bitcast.153, bf16[64,2,32,1536]{3,0,1,2:T(8,128)(2,1)} %copy-done.3, f32[32]{0:T(128)S(1)} %compare_convert_fusion), kind=kOutput, calls=%fused_computation.28 | convolution fusion | flops 3222274048 | bytes 15204480 | tf_op jit(solution)/shard_map/icth,chm->mit/dot_general | solution.py:66
  43.6 2.2 copy.105
  45.8 1.7 reshape.237
  47.5 32.0 %all_to_all.33 = bf16[4,2,65536]{2,1,0:T(2,128)(2,1)} all-to-all(bf16[4,2,65536]{2,1,0:T(2,128)(2,1)S(1)} %reshape.237), channel_id=1, replica_groups=mesh['grp'=2,'chan'=4,'sub'=4] {'chan'}, dimensions={0} | all-to-all | bytes 2097152 | tf_op jit(solution)/shard_map/all_to_all | solution.py:70
  79.5 3.1 reshape.238
  82.6 6.5 %copy.149 = bf16[2,32,4,64,32]{4,1,3,2,0:T(8,128)(2,1)} copy(bf16[2,32,4,64,32]{3,4,0,1,2:T(8,128)(2,1)S(1)} %bitcast.149) | data formatting | bytes 2097152 | tf_op jit(solution)/shard_map/all_to_all | solution.py:70
  89.1 4.3 scatter_custom_fusion
  94.5 4.2 negate_convert_fusion
  98.7 1.3 maximum_maximum_fusion.1
  99.9 94.3 %all-gather.2.cloned.1.call-done = bf16[2,32,1024,32]{3,1,2,0:T(8,128)(2,1)} async-done(((bf16[2,32,256,32]{3,1,2,0:T(8,128)(2,1)}), bf16[2,32,1024,32]{3,1,2,0:T(8,128)(2,1)}) %all-gather.2.cloned.1.call-update) | async-done | bytes 4194320 | tf_op jit(solution)/shard_map/all_gather | solution.py:71
  194.3 19.1 %gather_fusion = bf16[1024,2,32,32]{3,2,1,0:T(8,128)(2,1)} fusion(bf16[2,32,1024,32]{3,1,2,0:T(8,128)(2,1)} %all-gather.2.cloned.1.call-done, s32[1024]{0:T(1024)S(1)} %broadcast_clamp_fusion), kind=kCustom, calls=%fused_computation | custom fusion | bytes 8392704 | tf_op jit(solution)/shard_map/jit(_take)/gather | solution.py:75
  213.4 17.5 %copy.109 = bf16[1024,2,32,32]{0,3,1,2:T(8,128)(2,1)} copy(bf16[1024,2,32,32]{3,2,1,0:T(8,128)(2,1)} %gather_fusion) | data formatting | bytes 8388608 | tf_op jit(solution)/shard_map/jit(_take)/gather | solution.py:75
  230.9 2.7 broadcast_select_fusion
  234.4 2.7 fusion.78
  237.0 31.6 %fusion.21 = f32[2,32,64,32]{2,3,0,1:T(8,128)S(1)} fusion(s32[32]{0:T(128)S(1)} %iota_add_fusion, s32[64,1024]{1,0:T(8,128)S(1)} %copy-done.8, bf16[1024,2,32,32]{0,3,1,2:T(8,128)(2,1)S(1)} %broadcast_select_fusion), kind=kOutput, calls=%fused_computation.35 | convolution fusion | flops 301989888 | bytes 4980864 | tf_op jit(solution)/shard_map/xbi,cxit->cxbt/dot_general | solution.py:91
  268.6 32.3 %fusion.18 = f32[2,32,64,32]{2,3,0,1:T(8,128)S(1)} fusion(s32[32]{0:T(128)S(1)} %iota_add_fusion, s32[64,1024]{1,0:T(8,128)S(1)} %copy-done.8, bf16[1024,2,32,32]{0,3,1,2:T(8,128)(2,1)S(1)} %broadcast_select_fusion), kind=kOutput, calls=%fused_computation.34 | convolution fusion | flops 301989888 | bytes 4980864 | tf_op jit(solution)/shard_map/xbi,cxit->cxbt/dot_general | solution.py:92
  301.3 1.2 convolution_convert_fusion
  302.4 3.1 reshape.203
  305.5 1.7 copy.194
  307.2 4.5 reshape.239
  311.7 4.6 all-to-all-start.1
  316.3 15.5 %convolution_bitcast_fusion = f32[32,1,256,1024]{3,2,0,1:T(8,128)} fusion(bf16[2,32,256,32]{2,3,0,1:T(8,128)(2,1)S(1)} %dynamic-slice_bitcast_fusion, bf16[1024,2,32,32]{0,3,1,2:T(8,128)(2,1)} %copy-done.1), kind=kOutput, calls=%fused_computation.8 | convolution fusion | flops 1073741824 | bytes 38797312 | tf_op jit(solution)/shard_map/cxit,cxjt->xij/dot_general | solution.py:78
  331.8 14.0 %fusion.14 = f32[32,256,1024]{2,1,0:T(8,128)} fusion(bf16[2,32,1024,32]{2,3,0,1:T(8,128)(2,1)S(1)} %copy-done.2, bf16[2,32,256,32]{2,3,0,1:T(8,128)(2,1)S(1)} %dynamic-slice_bitcast_fusion), kind=kOutput, calls=%fused_computation.26 | convolution fusion | flops 536870912 | bytes 36175872 | tf_op jit(solution)/shard_map/xit,xjt->xij/dot_general | solution.py:79
  345.8 21.7 %subtract_bitcast_fusion = f32[32,1,256,1024]{3,2,0,1:T(8,128)} fusion(f32[32,256,1024]{2,1,0:T(8,128)} %fusion.14, bf16[2,32,1024,32]{2,3,0,1:T(8,128)(2,1)S(1)} %copy-done.2, bf16[2,32,256,32]{2,3,0,1:T(8,128)(2,1)S(1)} %dynamic-slice_bitcast_fusion), kind=kOutput, calls=%fused_computation.4 | convolution fusion | flops 545259520 | bytes 69730304 | tf_op jit(solution)/shard_map/xit,xjt->xij/dot_general | solution.py:80
  367.5 33.5 %fusion = bf16[32,2,256,1024]{3,2,0,1:T(8,128)(2,1)} fusion(f32[32,1,256,1024]{3,2,0,1:T(8,128)} %subtract_bitcast_fusion, f32[32,1,256,1024]{3,2,0,1:T(8,128)} %convolution_bitcast_fusion, f32[]{:T(128)} %convert_reduce_fusion.1), kind=kLoop, calls=%fused_computation.3 | loop fusion | flops 50331648 | bytes 100663296 | tf_op jit(solution)/shard_map/convert_element_type | solution.py:83
  401.0 23.2 %copy.126 = bf16[32,2,256,1024]{3,2,1,0:T(8,128)(2,1)} copy(bf16[32,2,256,1024]{3,2,0,1:T(8,128)(2,1)} %fusion) | data formatting | bytes 67108864
  424.3 1.1 reshape.240
  425.4 1.8 bitcast_bitcast_fusion
  427.2 5.2 %copy.112 = bf16[1,32,2,4,32,32]{4,3,5,2,1,0:T(4,128)(2,1)S(1)} copy(bf16[1,32,2,4,32,32]{1,5,4,2,3,0:T(8,128)(2,1)} %bitcast_bitcast_fusion) | data formatting | bytes 1048576 | tf_op jit(solution)/shard_map/all_to_all | solution.py:107
  432.4 1.1 reshape.229
  433.5 7.3 %convolution_bitcast_fusion.1 = f32[32,32,2,12,128]{4,1,3,2,0:T(8,128)} fusion(bf16[2,12,128,2,128]{4,2,1,0,3:T(8,128)(2,1)} %bitcast.152, bf16[32,2,128,32,1,1]{2,3,1,0,4,5:T(8,128)(2,1)S(1)} %reshape.229), kind=kOutput, calls=%fused_computation.16 | convolution fusion | flops 1610612736 | bytes 14680064 | tf_op jit(solution)/shard_map/pcht,mch->ptm/dot_general | solution.py:33
  440.8 9.1 %slice_bitcast_fusion.15 = (f32[32,32,2,128]{3,1,2,0:T(8,128)S(1)}, f32[32,32,2,128]{3,1,2,0:T(8,128)S(1)}, f32[32,32,2,128]{3,1,2,0:T(8,128)S(1)}, f32[32,32,2,...) fusion(f32[32,32,2,12,128]{4,1,3,2,0:T(8,128)} %convolution_bit, ...), kind=kLoop, calls=%fused_computation.54 | loop fusion | bytes 25165824 | tf_op jit(solution)/shard_map/squeeze | solution.py:38
  449.9 5.0 %add_bitcast_fusion = f32[32,2,43,128]{3,2,1,0:T(8,128)S(1)} fusion(f32[32,32,2,128]{3,1,2,0:T(8,128)} %get-tuple-element.22, f32[32,32,2,128]{3,1,2,0:T(8,128)} %get-tuple-element.23, f32[32,32,2,128]{3,1,2,0:T(8,128)S(1)} %get-tuple-element.13, f32[32,32,2,128]{3,1,2,0:T(8,128)S(1)} %get-tuple-element.14, f32[32,32,2,128]{3,1,2,0:T(8,128)S(1)} %get-tuple-element.15, ...), kind=kLoop, calls=%fused_computation.33 | loop fusion | flops 3874816 | bytes 13991936 | tf_op jit(solution)/shard_map/transpose | solution.py:40
  454.9 1.8 reshape.234
  (39 shorter events, 5.0 us)
Async XLA Ops:
  7.2 187.1 %all-gather.2.cloned.1.call-start = ((), (), s32[]{:S(2)}) async-start(), calls=%async_computation.2 | async-start | bytes 20971520 | tf_op jit(solution)/shard_map/all_gather | solution.py:71
  11.7 4.2 copy-start.4
  29.8 4.8 %copy-start.3 = (bf16[64,2,32,1536]{3,0,1,2:T(8,128)(2,1)}, bf16[64,2,32,1536]{3,0,1,2:T(8,128)(2,1)S(1)}, u32[]{:S(2)}) copy-start(bf16[64,2,32,1536]{3,0,1,2:T(8,128)(2,1)S(1)} %copy_dynamic-update-slice_fusion) | copy-start | bytes 37748740
  82.6 6.6 %copy-start.5 = (s32[1024]{0:T(1024)S(1)}, s32[1024]{0:T(1024)}, u32[]{:S(2)}) copy-start(s32[1024]{0:T(1024)} %param.8) | copy-start | bytes 12292
  82.6 10.9 %copy-start.7 = (s32[256,1]{0,1:T(1,128)S(1)}, s32[256,1]{0,1:T(1,128)}, u32[]{:S(2)}) copy-start(s32[256,1]{0,1:T(1,128)} %param.11) | copy-start | bytes 3076
  82.6 11.0 %copy-start.6 = (s32[4]{0:T(128)S(1)}, s32[4]{0:T(128)}, u32[]{:S(2)}) copy-start(s32[4]{0:T(128)} %param.9) | copy-start | bytes 52
  230.9 3.4 copy-start
  234.4 66.5 %copy-start.1 = (bf16[1024,2,32,32]{0,3,1,2:T(8,128)(2,1)}, bf16[1024,2,32,32]{0,3,1,2:T(8,128)(2,1)S(1)}, u32[]{:S(2)}) copy-start(bf16[1024,2,32,32]{0,3,1,2:T(8,128)(2,1)S(1)} %broadcast_select_fusion) | copy-start | bytes 12582916
  234.4 2.7 copy-start.8
  311.7 112.5 %all-to-all-start.1 = ((bf16[4,2,32768]{2,1,0:T(2,128)(2,1)}), bf16[4,2,32768]{2,1,0:T(2,128)(2,1)S(1)}, u32[]{:S(2)}, u32[]{:S(2)}) async-start(bf16[4,2,32768]{2,1,0:T(2,128)(2,1)} %reshape.239), calls=%async_computation.1 | async-start | bytes 1048576 | tf_op jit(solution)/shard_map/all_to_all | solution.py:107
  316.3 15.5 %copy-start.2 = (bf16[2,32,1024,32]{2,3,0,1:T(8,128)(2,1)S(1)}, bf16[2,32,1024,32]{2,3,0,1:T(8,128)(2,1)}, u32[]{:S(2)}) copy-start(bf16[2,32,1024,32]{2,3,0,1:T(8,128)(2,1)} %fusion.78) | copy-start | bytes 12582916
Sparse Core Ops, SparseCore 0:
  89.2 104.9 all-gather.1
where the time goes:
time: 469 us; the launch traced here: 464 us
  matrix products  132 us (28%)
  local copies, waits for them, and re-layouts  131 us (28%)
  waiting for transfers between devices  94.4 us (20%)
  other arithmetic  55 us (12%)
  blocking collectives  32 us (7%)
  between operations  14.6 us (3%)
    all_gather x1, waiting for transfers between devices, local(): gathered = lax.all_gather(turned, 'sub', axis=2, tiled=True)  94.3 us
    unnamed x34, local copies, waits for them, and re-layouts  48.3 us
    gather x2, local copies, waits for them, and re-layouts, local(): by_id = jnp.take(gathered, order, axis=2)  36.6 us
    convert_element_type x1, other arithmetic, local(): (jnp.stack([real_part, imag_part], axis=1) / total).astype(jnp.bfloat16)  33.5 us
    dot_general x1, matrix products, local(): jnp.einsum('xbi,cxit->cxbt', weight_sin, by_id, preferred_element_type=jn...  32.3 us
    all_to_all x1, blocking collectives, local(): lax.all_to_all(spectra, 'chan', split_axis=1, concat_axis=2, tiled=True)  32 us
    dot_general x1, matrix products, local(): jnp.einsum('xbi,cxit->cxbt', weight_cos, by_id, preferred_element_type=jn...  31.6 us
    dot_general x1, matrix products, local(): jnp.einsum('xit,xjt->xij', mine[0], by_id[1], preferred_element_type=jnp....  21.7 us
  transfers between devices with their start and end apart: 2, of which 1 were waited for; matrix products, arithmetic and copies ran while one was open for 26% of the time, Pallas kernels for 0%

commit v1 on v0

--- a/solution.py
+++ b/solution.py
@@ -1,8 +1,11 @@
+import functools
 import math
 
 import jax
 import jax.numpy as jnp
 from jax import lax
+from jax.experimental import pallas as pl
+from jax.experimental.pallas import tpu as pltpu
 from jax.sharding import PartitionSpec as P
 
 NCH = 128
@@ -42,7 +45,7 @@
     )
 
 
-def local(voltages, taps, input_id, counts, delays, beam_owner):
+def local_plain(voltages, taps, input_id, counts, delays, beam_owner):
     n_chan = lax.axis_size("chan")
     n_sub = lax.axis_size("sub")
     inp_dev = voltages.shape[0]
@@ -112,6 +115,414 @@
     return (visibility, resynth)
 
 
+def filter_kernel(rows, pairs, steps, wide, n_chan, fr_ref, w_ref, mask_ref, out_ref):
+    group = 4 if pairs % 4 == 0 else 1
+    width = wide // n_chan
+    for first in range(0, pairs, group):
+        acc = jnp.zeros((group * rows, wide), jnp.float32)
+        for k in range(steps):
+            start = (first + k // 2) * rows
+            acc = acc + jnp.dot(
+                fr_ref[k % 2, start : start + group * rows, :],
+                w_ref[k],
+                preferred_element_type=jnp.float32,
+            )
+        for j in range(group):
+            pair = first + j
+            part = (acc[j * rows : (j + 1) * rows] * mask_ref[pair : pair + 1, :]).astype(
+                jnp.bfloat16
+            )
+            for d in range(n_chan):
+                out_ref[d, :, pair * width : (pair + 1) * width] = part[
+                    :, d * width : (d + 1) * width
+                ]
+
+
+def channelize(voltages, taps, valid, n_chan):
+    rows = voltages.shape[0]
+    spectra_n = valid.shape[0]
+    pairs = spectra_n // 2
+    chans, ch_dev = NCH, NCH // n_chan
+    steps = TAPS + 1
+    frames_n = spectra_n + TAPS - 1
+    frames = voltages.reshape(rows, 2, frames_n, chans)
+    frames = jnp.transpose(frames, (2, 0, 1, 3)).reshape(frames_n, rows, 2 * chans)
+    frames = jnp.pad(frames, ((0, frames_n % 2), (0, 0), (0, 0)))
+    frames = frames.reshape(-1, 2, rows, 2 * chans)
+    frames = jnp.transpose(frames, (1, 0, 2, 3)).reshape(2, -1, 2 * chans)
+    wide = 4 * chans
+    column = jnp.arange(wide, dtype=jnp.int32)
+    dest, rest = column // (4 * ch_dev), column % (4 * ch_dev)
+    parity, part, inner = rest // (2 * ch_dev), rest // ch_dev % 2, rest % ch_dev
+    channel = dest * ch_dev + inner
+    row = jnp.arange(2 * chans, dtype=jnp.int32)
+    phase = (row[:, None] % chans * channel[None, :] % chans).astype(jnp.float32) * (
+        2.0 * math.pi / chans
+    )
+    cosine, sine = jnp.cos(phase), jnp.sin(phase)
+    lower = row[:, None] >= chans
+    trig = jnp.where(
+        lower == (part[None, :] == 1), cosine, jnp.where(lower, sine, -sine)
+    )
+    trig = lax.optimization_barrier(trig)
+    taps2 = taps.reshape(TAPS, chans)
+    taps2 = jnp.concatenate([taps2, taps2], axis=1)
+    even = jnp.pad(taps2, ((0, 1), (0, 0)))
+    odd = jnp.pad(taps2, ((1, 0), (0, 0)))
+    factor = jnp.where(parity[None, None, :] == 0, even[:, :, None], odd[:, :, None])
+    weights = (trig[None] * factor).astype(jnp.bfloat16)
+    mask = jnp.where(parity[None, :] == 0, valid[0::2, None], valid[1::2, None])
+    return pl.pallas_call(
+        functools.partial(filter_kernel, rows, pairs, steps, wide, n_chan),
+        out_shape=jax.ShapeDtypeStruct((n_chan, rows, spectra_n * 2 * ch_dev), jnp.bfloat16),
+        name="filterbank",
+    )(frames, weights, mask)
+
+
+def turn_kernel(n_chan, n_sub, pieces, x_ref, g_ref, own_sem, zs, zr, xs, xr, cs, cr):
+    me_c, me_s = lax.axis_index("chan"), lax.axis_index("sub")
+    core, across = me_s % 2, me_s // 2
+    n_x = n_sub // 2
+    twin = me_s + 1 - 2 * core
+    rows = x_ref.shape[1] // pieces
+    mesh_id = pl.DeviceIdType.MESH
+
+    def chan_of(offset):
+        return (me_c + offset) % n_chan
+
+    def sub_of(offset):
+        return (across + offset) % n_x * 2 + core
+
+    barrier = pltpu.get_barrier_semaphore()
+    for j in range(1, n_chan):
+        pl.semaphore_signal(barrier, device_id={"chan": chan_of(j)}, device_id_type=mesh_id)
+    for j in range(1, n_x):
+        pl.semaphore_signal(barrier, device_id={"sub": sub_of(j)}, device_id_type=mesh_id)
+    pl.semaphore_signal(barrier, device_id={"sub": twin}, device_id_type=mesh_id)
+    pl.semaphore_wait(barrier, n_chan + n_x - 1)
+
+    def place(ref, piece):
+        return ref.at[piece * rows : (piece + 1) * rows]
+
+    def z_copy(j, h):
+        return pltpu.make_async_remote_copy(
+            src_ref=place(x_ref.at[chan_of(j)], h),
+            dst_ref=place(g_ref.at[me_s, me_c], h),
+            send_sem=zs.at[j, h],
+            recv_sem=zr.at[j, h],
+            device_id={"chan": chan_of(j)},
+            device_id_type=mesh_id,
+        )
+
+    def source(sub, j, h):
+        if j == 0:
+            return place(x_ref.at[me_c], h)
+        return place(g_ref.at[sub, chan_of(n_chan - j)], h)
+
+    def x_copy(dx, j, h):
+        return pltpu.make_async_remote_copy(
+            src_ref=source(me_s, j, h),
+            dst_ref=place(g_ref.at[me_s, chan_of(n_chan - j)], h),
+            send_sem=xs.at[dx, j, h],
+            recv_sem=xr.at[dx, j, h],
+            device_id={"sub": sub_of(dx)},
+            device_id_type=mesh_id,
+        )
+
+    def core_copy(dx, j, h):
+        home = sub_of(n_x - dx)
+        block = place(g_ref.at[home, chan_of(n_chan - j)], h)
+        return pltpu.make_async_remote_copy(
+            src_ref=source(me_s, j, h) if dx == 0 else block,
+            dst_ref=block,
+            send_sem=cs.at[dx, j, h],
+            recv_sem=cr.at[dx, j, h],
+            device_id={"sub": twin},
+            device_id_type=mesh_id,
+        )
+
+    own = pltpu.make_async_copy(x_ref.at[me_c], g_ref.at[me_s, me_c], own_sem)
+    started = []
+    for h in range(pieces):
+        for j in range(1, n_chan):
+            copy = z_copy(j, h)
+            copy.start()
+            started.append(copy)
+    own.start()
+
+    def spread(j, h):
+        for dx in range(1, n_x):
+            copy = x_copy(dx, j, h)
+            copy.start()
+            started.append(copy)
+        copy = core_copy(0, j, h)
+        copy.start()
+        started.append(copy)
+
+    for h in range(pieces):
+        spread(0, h)
+    order = [(j, h) for h in range(pieces) for j in range(1, n_chan)]
+    relay = [(j, h) for h in range(pieces) for j in range(n_chan)]
+    for j, h in order:
+        z_copy(j, h).wait_recv()
+        spread(j, h)
+    for j, h in relay:
+        for dx in range(1, n_x):
+            x_copy(dx, j, h).wait_recv()
+            copy = core_copy(dx, j, h)
+            copy.start()
+            started.append(copy)
+    for j, h in relay:
+        for dx in range(n_x):
+            core_copy(dx, j, h).wait_recv()
+    for copy in started:
+        copy.wait_send()
+    own.wait()
+
+
+def corner_turn(blocks, n_chan, n_sub):
+    pieces = 2
+    dma = pltpu.SemaphoreType.DMA
+    n_x = n_sub // 2
+    return pl.pallas_call(
+        functools.partial(turn_kernel, n_chan, n_sub, pieces),
+        out_shape=jax.ShapeDtypeStruct((n_sub,) + blocks.shape, jnp.bfloat16),
+        in_specs=[pl.BlockSpec(memory_space=pltpu.VMEM)],
+        out_specs=pl.BlockSpec(memory_space=pl.ANY),
+        scratch_shapes=[
+            dma,
+            dma((n_chan, pieces)),
+            dma((n_chan, pieces)),
+            dma((n_x, n_chan, pieces)),
+            dma((n_x, n_chan, pieces)),
+            dma((n_x, n_chan, pieces)),
+            dma((n_x, n_chan, pieces)),
+        ],
+        compiler_params=pltpu.CompilerParams(collective_id=0, has_side_effects=True),
+        name="corner_turn",
+    )(blocks)
+
+
+def beam_kernel(ch_dev, spectra_n, n_chan, first_ref, g_ref, perm_ref, delay_ref, cos_ref, sin_ref, sel_ref, id_ref, out_ref, held):
+    step = pl.program_id(0)
+
+    @pl.when(step == 0)
+    def _():
+        wide = min(256, g_ref.shape[1])
+
+        @pl.loop(0, g_ref.shape[1] // wide)
+        def _(m):
+            at = pl.multiple_of(m * wide, wide)
+            sorted_part = lax.dot_general(
+                g_ref[:, pl.ds(at, wide)],
+                perm_ref[...],
+                (((0,), (0,)), ((), ())),
+                preferred_element_type=jnp.float32,
+            )
+            for tile in range(held.shape[0]):
+                held[tile, pl.ds(at, wide), :] = sorted_part[:, tile * 128 : (tile + 1) * 128]
+
+    def rows_of(start):
+        every = pl.ds(start, spectra_n, stride=2 * ch_dev)
+        return jnp.concatenate([held[tile, every, :] for tile in range(held.shape[0])], axis=1)
+
+    both = jnp.concatenate([rows_of(step), rows_of(step + ch_dev)], axis=0).astype(jnp.bfloat16)
+    id_ref[0] = both
+    channel = first_ref[0] + step
+    index = (delay_ref[...] * channel) & (NCH - 1)
+    beams_n, inputs = index.shape
+    cosine = jnp.broadcast_to(cos_ref[...], (beams_n, NCH))
+    sine = jnp.broadcast_to(sin_ref[...], (beams_n, NCH))
+
+    def look(table):
+        parts = [
+            jnp.take_along_axis(table, index[:, at : at + NCH], axis=1, mode="promise_in_bounds")
+            for at in range(0, inputs, NCH)
+        ]
+        return jnp.concatenate(parts, axis=1).astype(jnp.bfloat16)
+
+    weights = jnp.concatenate([look(cosine), look(sine)], axis=0)
+    mixed = lax.dot_general(
+        weights, both, (((1,), (1,)), ((), ())), preferred_element_type=jnp.float32
+    )
+    upper, lower = mixed[:beams_n], mixed[beams_n:]
+    beam_re = upper[:, :spectra_n] - lower[:, spectra_n:]
+    beam_im = upper[:, spectra_n:] + lower[:, :spectra_n]
+    beams = jnp.concatenate([beam_re, beam_im], axis=1).astype(jnp.bfloat16)
+    placed = jnp.dot(sel_ref[...], beams, preferred_element_type=jnp.float32).astype(jnp.bfloat16)
+    out_ref[:, 0] = placed.reshape(n_chan, placed.shape[0] // n_chan, placed.shape[1])
+
+
+def form_beams(gathered, perm, delays, tables, select, first, ch_dev, spectra_n, n_chan):
+    inputs = perm.shape[0]
+    slots, beams_n = select.shape
+    whole = lambda shape: pl.BlockSpec(shape, lambda f, s: (0,) * len(shape), pipeline_mode=pl.Buffered(1))
+    cols = gathered.shape[1]
+    return pl.pallas_call(
+        functools.partial(beam_kernel, ch_dev, spectra_n, n_chan),
+        grid_spec=pltpu.PrefetchScalarGridSpec(
+            num_scalar_prefetch=1,
+            grid=(ch_dev,),
+            in_specs=[
+                whole((inputs, cols)),
+                whole((inputs, inputs)),
+                whole((beams_n, inputs)),
+                whole((1, NCH)),
+                whole((1, NCH)),
+                whole((slots, beams_n)),
+            ],
+            out_specs=[
+                pl.BlockSpec((1, 2 * spectra_n, inputs), lambda f, s: (f, 0, 0)),
+                pl.BlockSpec((n_chan, 1, slots // n_chan, 2 * spectra_n), lambda f, s: (0, f, 0, 0)),
+            ],
+            scratch_shapes=[pltpu.VMEM((inputs // 128, cols, 128), jnp.float32)],
+        ),
+        out_shape=[
+            jax.ShapeDtypeStruct((ch_dev, 2 * spectra_n, inputs), jnp.bfloat16),
+            jax.ShapeDtypeStruct((n_chan, ch_dev, slots // n_chan, 2 * spectra_n), jnp.bfloat16),
+        ],
+        compiler_params=pltpu.CompilerParams(dimension_semantics=("arbitrary",)),
+        name="beams",
+    )(first, gathered, perm, delays, *tables, select)
+
+
+def visibility_kernel(sub_ref, scale_ref, left_ref, right_ref, out_ref):
+    for j in range(left_ref.shape[0]):
+        left = left_ref[j]
+        half, rows = left.shape[0] // 2, left.shape[1]
+        turned = jnp.concatenate([left[half:], -left[:half]], axis=0)
+        both = jnp.concatenate([left, turned], axis=1)
+        product = lax.dot_general(
+            both, right_ref[j], (((0,), (0,)), ((), ())), preferred_element_type=jnp.float32
+        )
+        product = (product * scale_ref[0]).astype(jnp.bfloat16)
+        out_ref[j, 0] = product[:rows]
+        out_ref[j, 1] = product[rows:]
+
+
+def correlate(by_id, scale, sub_index, rows):
+    ch_dev, depth, inputs = by_id.shape
+    group = 2 if ch_dev % 2 == 0 else 1
+    return pl.pallas_call(
+        visibility_kernel,
+        grid_spec=pltpu.PrefetchScalarGridSpec(
+            num_scalar_prefetch=1,
+            grid=(ch_dev // group,),
+            in_specs=[
+                pl.BlockSpec(memory_space=pltpu.SMEM),
+                pl.BlockSpec((group, depth, rows), lambda f, s: (f, 0, s[0])),
+                pl.BlockSpec((group, depth, inputs), lambda f, s: (f, 0, 0)),
+            ],
+            out_specs=pl.BlockSpec((group, 2, rows, inputs), lambda f, s: (f, 0, 0, 0)),
+        ),
+        out_shape=jax.ShapeDtypeStruct((ch_dev, 2, rows, inputs), jnp.bfloat16),
+        cost_estimate=pl.CostEstimate(
+            flops=4 * ch_dev * rows * inputs * depth,
+            bytes_accessed=4 * ch_dev * rows * inputs,
+            transcendentals=0,
+        ),
+        name="visibility",
+    )(sub_index, scale, by_id, by_id)
+
+
+def voice_kernel(spectra_n, count, frames_n, b_ref, w_ref, out_ref):
+    chans = w_ref.shape[2] // 2
+    group = 4
+    for first in range(0, frames_n, group):
+        size = min(group, frames_n - first)
+        acc = jnp.zeros((size * count, w_ref.shape[2]), jnp.float32)
+        for k in range(TAPS):
+            low = first - k
+            if low + size <= 0 or low >= spectra_n:
+                continue
+            start = (low + TAPS - 1) * count
+            acc = acc + jnp.dot(
+                b_ref[start : start + size * count, :], w_ref[k], preferred_element_type=jnp.float32
+            )
+        for j in range(size):
+            at = (first + j) * chans
+            for c in range(2):
+                out_ref[c, :, at : at + chans] = acc[
+                    j * count : (j + 1) * count, c * chans : (c + 1) * chans
+                ]
+
+
+def synthesize(received, taps):
+    chans, count, _ = received.shape
+    spectra_n = received.shape[2] // 2
+    frames_n = spectra_n + TAPS - 1
+    bank = received.reshape(chans, count, 2, spectra_n)
+    bank = jnp.transpose(bank, (3, 1, 2, 0)).reshape(spectra_n, count, 2 * chans)
+    bank = jnp.pad(bank, ((TAPS - 1, TAPS - 1), (0, 0), (0, 0))).reshape(-1, 2 * chans)
+    index = jnp.arange(2 * chans, dtype=jnp.int32)
+    inner = index % chans
+    phase = (inner[:, None] * inner[None, :] % chans).astype(jnp.float32) * (2.0 * math.pi / chans)
+    cosine, sine = jnp.cos(phase), jnp.sin(phase)
+    from_im, to_im = index[:, None] >= chans, index[None, :] >= chans
+    trig = jnp.where(from_im == to_im, cosine, jnp.where(to_im, sine, -sine))
+    trig = lax.optimization_barrier(trig)
+    taps2 = taps.reshape(TAPS, 1, chans)
+    weights = (trig[None] * jnp.concatenate([taps2, taps2], axis=2)).astype(jnp.bfloat16)
+    voices = pl.pallas_call(
+        functools.partial(voice_kernel, spectra_n, count, frames_n),
+        out_shape=jax.ShapeDtypeStruct((2, count, frames_n * chans), jnp.float32),
+        name="voices",
+    )(bank, weights)
+    return jnp.transpose(voices, (1, 0, 2))
+
+
+def local(voltages, taps, input_id, counts, delays, beam_owner):
+    n_chan = lax.axis_size("chan")
+    n_sub = lax.axis_size("sub")
+    inp_dev = voltages.shape[0]
+    inputs = input_id.shape[0]
+    chans = NCH
+    spectra_n = BLOCKS * SPEC
+    ch_dev = chans // n_chan
+    rows = inputs // n_sub
+    section = BEAMS // n_sub
+    most = min(section, max(2, 2 * section // n_chan))
+    if inp_dev % 32 or 4 * ch_dev % 128 or rows % 128 or n_sub % 2 or most % 16:
+        return local_plain(voltages, taps, input_id, counts, delays, beam_owner)
+    position = jnp.arange(spectra_n, dtype=jnp.int32)
+    valid = (position % SPEC < jnp.repeat(counts, SPEC)).astype(jnp.float32)
+    total = jnp.sum(counts.astype(jnp.float32))
+    chan_index, sub_index = lax.axis_index("chan"), lax.axis_index("sub")
+    blocks = channelize(voltages, taps, valid, n_chan)
+    gathered = corner_turn(blocks, n_chan, n_sub).reshape(inputs, -1)
+    names = jnp.transpose(input_id.reshape(n_chan, n_sub, inp_dev), (1, 0, 2)).reshape(inputs)
+    perm = (names[:, None] == jnp.arange(inputs, dtype=jnp.int32)[None, :]).astype(jnp.bfloat16)
+    angle = jnp.arange(chans, dtype=jnp.int32).astype(jnp.float32) * (2.0 * math.pi / chans)
+    scale = 1.0 / math.sqrt(inputs)
+    tables = [
+        (wave(angle) * scale).astype(jnp.bfloat16).astype(jnp.float32)[None, :]
+        for wave in (jnp.cos, jnp.sin)
+    ]
+    owner = lax.dynamic_slice_in_dim(beam_owner[:, 0], sub_index * section, section)
+    beam = jnp.arange(section, dtype=jnp.int32)
+    earlier = (owner[None, :] == owner[:, None]) & (beam[None, :] < beam[:, None])
+    rank = jnp.sum(earlier.astype(jnp.int32), axis=1)
+    target = owner * most + rank
+    select = (jnp.arange(n_chan * most, dtype=jnp.int32)[:, None] == target[None, :]).astype(
+        jnp.bfloat16
+    )
+    by_id, placed = form_beams(
+        gathered,
+        perm,
+        delays,
+        tables,
+        select,
+        (chan_index * ch_dev).astype(jnp.int32)[None],
+        ch_dev,
+        spectra_n,
+        n_chan,
+    )
+    received = lax.all_to_all(placed, "chan", split_axis=0, concat_axis=0, tiled=True)
+    visibility = correlate(by_id, (1.0 / total)[None], sub_index.astype(jnp.int32)[None], rows)
+    resynth = synthesize(received.reshape(chans, most, 2 * spectra_n), taps)
+    return (visibility, resynth)
+
+
 def solution(mesh):
     placed = (
         P(("grp", "chan", "sub"), None, None),

time: 469 us -> 146 us (0.31)
  matrix products: 132 us -> 0 us
  local copies, waits for them, and re-layouts: 131 us -> 21.6 us
  Pallas kernels: 0 us -> 102 us
  waiting for transfers between devices: 94.4 us -> 0.01 us
  other arithmetic: 55 us -> 13.2 us
  blocking collectives: 32 us -> 0 us
  between operations: 14.6 us -> 1.51 us
    dot_general x8 -> x0, matrix products: 132 us -> none  [the longest x1 32.3 us: local(): jnp.einsum('xbi,cxit->cxbt', weight_sin, by_id, preferred_element_type=jn...]
    pallas_call x0 -> x5, Pallas kernels: none -> 102 us  [the longest x1 37.1 us: corner_turn(): pl.pallas_call(functools.partial(turn_kernel, n_chan, n_sub, pieces), out...]
    all_gather x1 -> x0, waiting for transfers between devices: 94.3 us -> none  [local(): gathered = lax.all_gather(turned, 'sub', axis=2, tiled=True)]
    unnamed x34 -> x11, local copies, waits for them, and re-layouts: 48.3 us -> 6.83 us
    gather x2 -> x0, local copies, waits for them, and re-layouts: 36.6 us -> none  [local(): by_id = jnp.take(gathered, order, axis=2)]
    all_to_all x1 -> x0, blocking collectives: 32 us -> none  [local(): lax.all_to_all(spectra, 'chan', split_axis=1, concat_axis=2, tiled=True)]
    convert_element_type x1 -> x5, other arithmetic: 33.5 us -> 6.81 us  [the longest x1 2.26 us: channelize(): weights = (trig[None] * factor).astype(jnp.bfloat16)]
    all_to_all x3 -> x0, local copies, waits for them, and re-layouts: 13.5 us -> none  [the longest x2 7.04 us: local(): lax.all_to_all(placed, 'chan', split_axis=0, concat_axis=3, tiled=True)[0]]
  transfers between devices with their start and end apart: 2 -> 1, of which waited for: 1 -> 0; matrix products, arithmetic and copies ran while one was open for 26% -> 2% of each run, Pallas kernels for 0% -> 13%
where the time goes in v1:
time: 146 us; the launch traced here: 145 us
  Pallas kernels  102 us (70%)
  local copies, waits for them, and re-layouts  21.6 us (15%)
  other arithmetic  13.2 us (9%)
  starting transfers between devices  7.15 us (5%)
  between operations  1.51 us (1%)
    pallas_call x1, Pallas kernels, corner_turn(): pl.pallas_call(functools.partial(turn_kernel, n_chan, n_sub, pieces), out...  37.1 us
    pallas_call x1, Pallas kernels, form_beams(): pl.pallas_call(functools.partial(beam_kernel, ch_dev, spectra_n, n_chan),...  33.5 us
    pallas_call x1, Pallas kernels, correlate(): pl.pallas_call(visibility_kernel, grid_spec=pltpu.PrefetchScalarGridSpec(...  19.5 us
    all_to_all x1, starting transfers between devices, local(): lax.all_to_all(placed, 'chan', split_axis=0, concat_axis=0, tiled=True)  7.15 us
    pallas_call x1, Pallas kernels, channelize(): pl.pallas_call(functools.partial(filter_kernel, rows, pairs, steps, wide,...  7.1 us
    unnamed x11, local copies, waits for them, and re-layouts  6.83 us
    pallas_call x1, Pallas kernels, synthesize(): pl.pallas_call(functools.partial(voice_kernel, spectra_n, count, frames_n...  4.72 us
    reshape x1, local copies, waits for them, and re-layouts, channelize(): frames = voltages.reshape(rows, 2, frames_n, chans)  3.68 us
  transfers between devices with their start and end apart: 1, of which 0 were waited for; matrix products, arithmetic and copies ran while one was open for 2% of the time, Pallas kernels for 13%

profile of v1, /device:TPU:0, one launch (start us, length us, event | category | flops | bytes accessed | tf_op | source)
XLA Modules:
  0.0 145.3 jit_solution(2184750045479459988)
XLA Ops:
  0.7 0.7 broadcast_in_dim.72
  1.4 0.1 reshape.235
  1.5 0.1 slice.6
  1.6 0.6 slice.7
  2.2 0.6 convert_convert_fusion
  2.9 0.7 dynamic-slice_bitcast_fusion
  3.6 0.2 convert_reduce_fusion
  3.8 0.7 multiply_add_fusion
  4.5 0.6 fusion.9.sel_ref
  5.1 2.2 %fusion.3 = f32[256,512]{1,0:T(8,128)S(1)} fusion(s32[512]{0:T(512)S(1)} %fusion.15, s32[256]{0:T(256)S(1)} %and_select_fusion.1, pred[512]{0:T(512)(128)(4,1)S(1)} %fusion.12, pred[256]{0:T(512)(128)(4,1)S(1)} %iota_compare_fusion.3), kind=kLoop, calls=%fused_computation.12 | loop fusion | flops 2359296 | bytes 528128 | tf_op jit(solution)/shard_map/jit(_where)/select_n | solution.py:164
  7.3 0.8 pad_maximum_fusion
  8.1 3.7 %reshape.241 = bf16[64,2,43,128]{3,2,1,0:T(8,128)(2,1)S(1)} reshape(bf16[64,2,5504]{2,1,0:T(2,128)(2,1)} %param.6) | data formatting | bytes 2818048 | tf_op jit(solution)/shard_map/reshape | solution.py:148
  11.8 1.5 %copy.23 = bf16[43,64,2,128]{3,2,1,0:T(2,128)(2,1)S(1)} copy(bf16[43,64,2,128]{3,0,2,1:T(8,128)(2,1)S(1)} %bitcast.25) | data formatting | bytes 2818048 | tf_op jit(solution)/shard_map/transpose | solution.py:149
  13.4 0.9 reshape.231
  14.3 0.0 copy-start.2
  14.3 0.1 pad.16
  14.5 1.2 copy.24
  15.7 0.0 copy-done.2
  15.7 0.7 broadcast_select_fusion.mask_ref
  16.4 2.3 %multiply_convert_fusion.w_ref = bf16[13,256,512]{2,1,0:T(8,128)(2,1)} fusion(f32[13,256]{1,0:T(8,128)S(1)} %get-tuple-element.15, f32[13,256]{1,0:T(8,128)S(1)} %get-tuple-element.14, f32[256,512]{1,0:T(8,128)S(1)} %fusion.3, pred[512]{0:T(512)(128)(4,1)S(1)} %fusion.17), kind=kLoop, calls=%fused_computation | loop fusion | flops 5111808 | bytes 3959296 | tf_op jit(solution)/shard_map/convert_element_type | solution.py:173
  18.6 7.1 %filterbank.1.x_ref = bf16[4,64,2048]{2,1,0:T(8,128)(2,1)} custom-call(bf16[2,1408,256]{2,1,0:T(8,128)(2,1)} %bitcast.27, bf16[13,256,512]{2,1,0:T(8,128)(2,1)} %multiply_convert_fusion.w_ref, f32[16,512]{1,0:T(8,128)} %broadcast_select_fusion.mask_ref), custom_call_target="tpu_custom_call" | custom-call | tf_op jit(solution)/shard_map/filterbank/pallas_call | solution.py:175
  25.7 0.0 copy-start.1
  25.7 37.1 %corner_turn.1 = bf16[4,4,64,2048]{3,2,1,0:T(8,128)(2,1)} custom-call(bf16[4,64,2048]{2,1,0:T(8,128)(2,1)} %filterbank.1.x_ref), custom_call_target="tpu_custom_call" | custom-call | tf_op jit(solution)/shard_map/corner_turn/pallas_call | solution.py:287
  62.8 0.0 copy-done.1
  62.8 0.1 reshape.237
  62.9 0.1 eq.113
  63.0 1.7 %fusion.perm_ref = bf16[1024,1024]{1,0:T(8,128)(2,1)} fusion(s32[1024]{0:T(1024)S(1)} %eq.113), kind=kLoop, calls=%fused_computation.2 | loop fusion | flops 2097152 | bytes 2101248 | tf_op jit(solution)/shard_map/convert_element_type | solution.py:494
  64.7 0.0 copy-start.3
  64.7 0.0 copy-start
  64.7 33.5 %beams.1 = (bf16[32,64,1024]{2,1,0:T(8,128)(2,1)}, bf16[4,32,32,64]{3,2,1,0:T(8,128)(2,1)}) custom-call(s32[1]{0:T(128)} %bitcast.2.first_ref, bf16[1024,2048]{1,0:T(8,128)(2,1)} %bitcast.24, bf16[1024,1024]{1,0:T(8,128)(2,1)} %fusion.perm_ref, s32[64,1024]{1,0:T(8,128)} %delay_ref.1, f32[1,128]{1,0:T(1,128)} %get-tuple-element.17.cos_ref, ...), custom_call_target="tpu_custom_call" | custom-call | tf_op jit(solution)/shard_map/beams/pallas_call | solution.py:361
  98.2 2.6 %reshape.243 = bf16[4,2,32768]{2,1,0:T(2,128)(2,1)} reshape(bf16[4,32,32,64]{3,2,1,0:T(8,128)(2,1)} %get-tuple-element.5) | data formatting | bytes 1048576
  100.8 7.1 %all-to-all-start = ((bf16[4,2,32768]{2,1,0:T(2,128)(2,1)}), bf16[4,2,32768]{2,1,0:T(2,128)(2,1)S(1)}, u32[]{:S(2)}, u32[]{:S(2)}) async-start(bf16[4,2,32768]{2,1,0:T(2,128)(2,1)} %reshape.243), calls=%async_computation | async-start | bytes 1048576 | tf_op jit(solution)/shard_map/all_to_all | solution.py:520
  107.9 1.1 fusion.7
  109.1 0.0 copy-done.3
  109.1 0.6 convert_reduce_fusion.1
  110.4 0.0 copy-done
  110.4 19.5 %visibility.1 = bf16[32,2,256,1024]{3,2,1,0:T(8,128)(2,1)} custom-call(s32[1]{0:T(128)} %bitcast.sub_ref, f32[1]{0:T(128)} %bitcast.1.scale_ref, bf16[32,64,1024]{2,1,0:T(8,128)(2,1)} %get-tuple-element.4.left_ref.right_ref, bf16[32,64,1024]{2,1,0:T(8,128)(2,1)} %get-tuple-element.4.left_ref.right_ref), custom_call_target="tpu_custom_call" | custom-call | flops 2147483648 | bytes 33554432 | tf_op jit(solution)/shard_map/visibility/pallas_call | solution.py:406
  129.9 1.6 %multiply_convert_fusion.1.w_ref = bf16[12,256,256]{2,1,0:T(8,128)(2,1)} fusion(f32[12,256]{1,0:T(8,128)S(1)} %maximum_bitcast_fusion, f32[256,256]{1,0:T(8,128)S(1)} %fusion.7), kind=kLoop, calls=%fused_computation.3 | loop fusion | flops 1572864 | bytes 1847296 | tf_op jit(solution)/shard_map/convert_element_type | solution.py:465
  131.5 0.0 all-to-all-done
  131.5 0.7 reshape.244
  132.2 0.8 reshape.242
  133.1 2.1 %copy.31 = bf16[128,32,2,32]{0,3,2,1:T(8,128)(2,1)S(1)} copy(bf16[128,32,2,32]{3,2,1,0:T(2,128)(2,1)S(1)} %reshape.242) | data formatting | bytes 1048576 | tf_op jit(solution)/shard_map/reshape;reshape | solution.py:454
  135.2 0.5 copy.27
  135.7 0.3 reshape.238
  136.1 1.0 pad.19
  137.1 4.7 %voices.1 = f32[2,32,5504]{2,1,0:T(8,128)} custom-call(bf16[1728,256]{1,0:T(8,128)(2,1)} %bitcast.29, bf16[12,256,256]{2,1,0:T(8,128)(2,1)} %multiply_convert_fusion.1.w_ref), custom_call_target="tpu_custom_call" | custom-call | tf_op jit(solution)/shard_map/voices/pallas_call | solution.py:466
  141.8 3.5 %copy.28 = f32[32,2,5504]{2,1,0:T(2,128)} copy(f32[32,2,5504]{2,0,1:T(8,128)} %bitcast.28) | data formatting | bytes 2818048
  (9 shorter events, 0.1 us)
Async XLA Ops:
  14.3 1.4 copy-start.2
  25.7 37.1 %copy-start.1 = (s32[1024]{0:T(1024)S(1)}, s32[1024]{0:T(1024)}, u32[]{:S(2)}) copy-start(s32[1024]{0:T(1024)} %param.8) | copy-start | bytes 12292
  64.7 44.4 %copy-start.3 = (s32[4]{0:T(128)S(1)}, s32[4]{0:T(128)}, u32[]{:S(2)}) copy-start(s32[4]{0:T(128)} %param.9) | copy-start | bytes 52
  64.7 45.7 %copy-start = (f32[1536]{0:T(1024)S(1)}, f32[1536]{0:T(1024)}, u32[]{:S(2)}) copy-start(f32[1536]{0:T(1024)} %param.7) | copy-start | bytes 18436
  100.8 30.7 %all-to-all-start = ((bf16[4,2,32768]{2,1,0:T(2,128)(2,1)}), bf16[4,2,32768]{2,1,0:T(2,128)(2,1)S(1)}, u32[]{:S(2)}, u32[]{:S(2)}) async-start(bf16[4,2,32768]{2,1,0:T(2,128)(2,1)} %reshape.243), calls=%async_computation | async-start | bytes 1048576 | tf_op jit(solution)/shard_map/all_to_all | solution.py:520

commit v2 on v1

--- a/solution.py
+++ b/solution.py
@@ -121,12 +121,14 @@
     for first in range(0, pairs, group):
         acc = jnp.zeros((group * rows, wide), jnp.float32)
         for k in range(steps):
-            start = (first + k // 2) * rows
-            acc = acc + jnp.dot(
-                fr_ref[k % 2, start : start + group * rows, :],
-                w_ref[k],
-                preferred_element_type=jnp.float32,
+            window = jnp.concatenate(
+                [
+                    jnp.concatenate([fr_ref[0, at], fr_ref[1, at]], axis=1)
+                    for at in range(2 * first + k, 2 * (first + group) + k, 2)
+                ],
+                axis=0,
             )
+            acc = acc + jnp.dot(window, w_ref[k], preferred_element_type=jnp.float32)
         for j in range(group):
             pair = first + j
             part = (acc[j * rows : (j + 1) * rows] * mask_ref[pair : pair + 1, :]).astype(
@@ -146,10 +148,7 @@
     steps = TAPS + 1
     frames_n = spectra_n + TAPS - 1
     frames = voltages.reshape(rows, 2, frames_n, chans)
-    frames = jnp.transpose(frames, (2, 0, 1, 3)).reshape(frames_n, rows, 2 * chans)
-    frames = jnp.pad(frames, ((0, frames_n % 2), (0, 0), (0, 0)))
-    frames = frames.reshape(-1, 2, rows, 2 * chans)
-    frames = jnp.transpose(frames, (1, 0, 2, 3)).reshape(2, -1, 2 * chans)
+    frames = jnp.transpose(frames, (1, 2, 0, 3))
     wide = 4 * chans
     column = jnp.arange(wide, dtype=jnp.int32)
     dest, rest = column // (4 * ch_dev), column % (4 * ch_dev)
@@ -179,7 +178,33 @@
     )(frames, weights, mask)
 
 
-def turn_kernel(n_chan, n_sub, pieces, x_ref, g_ref, own_sem, zs, zr, xs, xr, cs, cr):
+def weigh(channel, scale, delay_ref, out_ref, f):
+    beams_n, inputs = delay_ref.shape
+    high, wide = 16, 512
+    unit = 2.0 * math.pi / NCH
+    quarter = NCH // 4
+
+    @pl.loop(0, beams_n // high)
+    def _(row):
+        at = pl.multiple_of(row * high, high)
+        for left in range(0, inputs, wide):
+            turn = (delay_ref[pl.ds(at, high), left : left + wide] * channel) & (NCH - 1)
+            quadrant = (turn + quarter // 2) >> (quarter.bit_length() - 1)
+            x = (turn - quadrant * quarter).astype(jnp.float32) * unit
+            y = x * x
+            even = 1.0 + y * (-1 / 2 + y * (1 / 24 + y * (-1 / 720 + y * (1 / 40320))))
+            odd = x * (1.0 + y * (-1 / 6 + y * (1 / 120 + y * (-1 / 5040 + y * (1 / 362880)))))
+            swap = (quadrant & 1) == 1
+            cosine = jnp.where(swap, odd, even) * scale
+            sine = jnp.where(swap, even, odd) * scale
+            cosine = jnp.where(((quadrant + 1) & 2) == 2, -cosine, cosine)
+            sine = jnp.where((quadrant & 2) == 2, -sine, sine)
+            out_ref[f, pl.ds(at, high), left : left + wide] = cosine.astype(jnp.bfloat16)
+            low = pl.multiple_of(at + beams_n, high)
+            out_ref[f, pl.ds(low, high), left : left + wide] = sine.astype(jnp.bfloat16)
+
+
+def turn_kernel(n_chan, n_sub, pieces, scale, x_ref, delay_ref, g_ref, weight_ref, own_sem, zs, zr, xs, xr, cs, cr):
     me_c, me_s = lax.axis_index("chan"), lax.axis_index("sub")
     core, across = me_s % 2, me_s // 2
     n_x = n_sub // 2
@@ -261,34 +286,61 @@
 
     for h in range(pieces):
         spread(0, h)
-    order = [(j, h) for h in range(pieces) for j in range(1, n_chan)]
-    relay = [(j, h) for h in range(pieces) for j in range(n_chan)]
-    for j, h in order:
-        z_copy(j, h).wait_recv()
-        spread(j, h)
-    for j, h in relay:
-        for dx in range(1, n_x):
-            x_copy(dx, j, h).wait_recv()
-            copy = core_copy(dx, j, h)
-            copy.start()
-            started.append(copy)
-    for j, h in relay:
-        for dx in range(n_x):
-            core_copy(dx, j, h).wait_recv()
+    ch_dev = weight_ref.shape[0]
+    slots = pieces * (2 * n_chan - 1)
+    share = -(-ch_dev * 4 // (3 * slots))
+    done = [0]
+
+    def work():
+        first, last = done[0], min(ch_dev, done[0] + share)
+        done[0] = last
+        if first < last:
+
+            @pl.loop(first, last)
+            def _(f):
+                weigh(me_c * ch_dev + f, scale, delay_ref, weight_ref, f)
+
+    def relay(h):
+        for j in range(n_chan):
+            work()
+            for dx in range(1, n_x):
+                x_copy(dx, j, h).wait_recv()
+                copy = core_copy(dx, j, h)
+                copy.start()
+                started.append(copy)
+
+    for h in range(pieces):
+        for j in range(1, n_chan):
+            work()
+            z_copy(j, h).wait_recv()
+            spread(j, h)
+        if h > 0:
+            relay(h - 1)
+    relay(pieces - 1)
+    while done[0] < ch_dev:
+        work()
+    for h in range(pieces):
+        for j in range(n_chan):
+            for dx in range(n_x):
+                core_copy(dx, j, h).wait_recv()
     for copy in started:
         copy.wait_send()
     own.wait()
 
 
-def corner_turn(blocks, n_chan, n_sub):
-    pieces = 2
+def corner_turn(blocks, delays, n_chan, n_sub):
+    pieces = 4
     dma = pltpu.SemaphoreType.DMA
     n_x = n_sub // 2
+    beams_n, inputs = delays.shape
     return pl.pallas_call(
-        functools.partial(turn_kernel, n_chan, n_sub, pieces),
-        out_shape=jax.ShapeDtypeStruct((n_sub,) + blocks.shape, jnp.bfloat16),
-        in_specs=[pl.BlockSpec(memory_space=pltpu.VMEM)],
-        out_specs=pl.BlockSpec(memory_space=pl.ANY),
+        functools.partial(turn_kernel, n_chan, n_sub, pieces, 1.0 / math.sqrt(inputs)),
+        out_shape=[
+            jax.ShapeDtypeStruct((n_sub,) + blocks.shape, jnp.bfloat16),
+            jax.ShapeDtypeStruct((NCH // n_chan, 2 * beams_n, inputs), jnp.bfloat16),
+        ],
+        in_specs=[pl.BlockSpec(memory_space=pltpu.VMEM)] * 2,
+        out_specs=[pl.BlockSpec(memory_space=pl.ANY), pl.BlockSpec(memory_space=pltpu.VMEM)],
         scratch_shapes=[
             dma,
             dma((n_chan, pieces)),
@@ -300,14 +352,23 @@
         ],
         compiler_params=pltpu.CompilerParams(collective_id=0, has_side_effects=True),
         name="corner_turn",
-    )(blocks)
-
-
-def beam_kernel(ch_dev, spectra_n, n_chan, first_ref, g_ref, perm_ref, delay_ref, cos_ref, sin_ref, sel_ref, id_ref, out_ref, held):
+    )(blocks, delays)
+
+
+def beam_kernel(ch_dev, spectra_n, n_chan, batch, g_ref, perm_ref, weight_ref, sel_ref, id_ref, out_ref, held, ready, own_sem, send, recv):
     step = pl.program_id(0)
+    pair = weight_ref.shape[0]
+    steps = ch_dev // pair
+    me_c = lax.axis_index("chan")
+    mesh_id = pl.DeviceIdType.MESH
 
     @pl.when(step == 0)
     def _():
+        barrier = pltpu.get_barrier_semaphore()
+        for j in range(1, n_chan):
+            pl.semaphore_signal(
+                barrier, device_id={"chan": (me_c + j) % n_chan}, device_id_type=mesh_id
+            )
         wide = min(256, g_ref.shape[1])
 
         @pl.loop(0, g_ref.shape[1] // wide)
@@ -322,68 +383,104 @@
             for tile in range(held.shape[0]):
                 held[tile, pl.ds(at, wide), :] = sorted_part[:, tile * 128 : (tile + 1) * 128]
 
+        pl.semaphore_wait(barrier, n_chan - 1)
+
     def rows_of(start):
         every = pl.ds(start, spectra_n, stride=2 * ch_dev)
         return jnp.concatenate([held[tile, every, :] for tile in range(held.shape[0])], axis=1)
 
-    both = jnp.concatenate([rows_of(step), rows_of(step + ch_dev)], axis=0).astype(jnp.bfloat16)
-    id_ref[0] = both
-    channel = first_ref[0] + step
-    index = (delay_ref[...] * channel) & (NCH - 1)
-    beams_n, inputs = index.shape
-    cosine = jnp.broadcast_to(cos_ref[...], (beams_n, NCH))
-    sine = jnp.broadcast_to(sin_ref[...], (beams_n, NCH))
-
-    def look(table):
-        parts = [
-            jnp.take_along_axis(table, index[:, at : at + NCH], axis=1, mode="promise_in_bounds")
-            for at in range(0, inputs, NCH)
-        ]
-        return jnp.concatenate(parts, axis=1).astype(jnp.bfloat16)
-
-    weights = jnp.concatenate([look(cosine), look(sine)], axis=0)
-    mixed = lax.dot_general(
-        weights, both, (((1,), (1,)), ((), ())), preferred_element_type=jnp.float32
-    )
-    upper, lower = mixed[:beams_n], mixed[beams_n:]
-    beam_re = upper[:, :spectra_n] - lower[:, spectra_n:]
-    beam_im = upper[:, spectra_n:] + lower[:, :spectra_n]
-    beams = jnp.concatenate([beam_re, beam_im], axis=1).astype(jnp.bfloat16)
+    def form(j):
+        f = step * pair + j
+        both = jnp.concatenate([rows_of(f), rows_of(f + ch_dev)], axis=0).astype(jnp.bfloat16)
+        id_ref[j] = both
+        mixed = lax.dot_general(
+            weight_ref[j], both, (((1,), (1,)), ((), ())), preferred_element_type=jnp.float32
+        )
+        beams_n = mixed.shape[0] // 2
+        upper, lower = mixed[:beams_n], mixed[beams_n:]
+        beam_re = upper[:, :spectra_n] - lower[:, spectra_n:]
+        beam_im = upper[:, spectra_n:] + lower[:, :spectra_n]
+        return [beam_re, beam_im]
+
+    beams = jnp.concatenate(form(0) + form(1), axis=1).astype(jnp.bfloat16)
     placed = jnp.dot(sel_ref[...], beams, preferred_element_type=jnp.float32).astype(jnp.bfloat16)
-    out_ref[:, 0] = placed.reshape(n_chan, placed.shape[0] // n_chan, placed.shape[1])
-
-
-def form_beams(gathered, perm, delays, tables, select, first, ch_dev, spectra_n, n_chan):
+    most = placed.shape[0] // n_chan
+    for d in range(n_chan):
+        ready[d, step] = placed[d * most : (d + 1) * most]
+
+    def copy_of(b, j):
+        to = (me_c + j) % n_chan
+        return pltpu.make_async_remote_copy(
+            src_ref=ready.at[to, pl.ds(b * batch, batch)],
+            dst_ref=out_ref.at[me_c, pl.ds(b * batch, batch)],
+            send_sem=send.at[b, j],
+            recv_sem=recv.at[b, j],
+            device_id={"chan": to},
+            device_id_type=mesh_id,
+        )
+
+    for b in range(steps // batch):
+
+        @pl.when(step == (b + 1) * batch - 1)
+        def _():
+            for j in range(1, n_chan):
+                copy_of(b, j).start()
+
+    @pl.when(step == steps - 1)
+    def _():
+        own = pltpu.make_async_copy(ready.at[me_c], out_ref.at[me_c], own_sem)
+        own.start()
+        for b in range(steps // batch):
+            for j in range(1, n_chan):
+                copy_of(b, j).wait_recv()
+        for b in range(steps // batch):
+            for j in range(1, n_chan):
+                copy_of(b, j).wait_send()
+        own.wait()
+
+
+def form_beams(gathered, perm, weights, select, spectra_n, n_chan):
     inputs = perm.shape[0]
+    ch_dev, double_n, _ = weights.shape
     slots, beams_n = select.shape
-    whole = lambda shape: pl.BlockSpec(shape, lambda f, s: (0,) * len(shape), pipeline_mode=pl.Buffered(1))
     cols = gathered.shape[1]
+    pair = 2
+    steps = ch_dev // pair
+    batch = steps // 4
+    dma = pltpu.SemaphoreType.DMA
+    whole = lambda shape: pl.BlockSpec(
+        shape, lambda f: (0,) * len(shape), pipeline_mode=pl.Buffered(1)
+    )
+    travel = (n_chan, steps, slots // n_chan, 2 * pair * spectra_n)
     return pl.pallas_call(
-        functools.partial(beam_kernel, ch_dev, spectra_n, n_chan),
-        grid_spec=pltpu.PrefetchScalarGridSpec(
-            num_scalar_prefetch=1,
-            grid=(ch_dev,),
-            in_specs=[
-                whole((inputs, cols)),
-                whole((inputs, inputs)),
-                whole((beams_n, inputs)),
-                whole((1, NCH)),
-                whole((1, NCH)),
-                whole((slots, beams_n)),
-            ],
-            out_specs=[
-                pl.BlockSpec((1, 2 * spectra_n, inputs), lambda f, s: (f, 0, 0)),
-                pl.BlockSpec((n_chan, 1, slots // n_chan, 2 * spectra_n), lambda f, s: (0, f, 0, 0)),
-            ],
-            scratch_shapes=[pltpu.VMEM((inputs // 128, cols, 128), jnp.float32)],
-        ),
+        functools.partial(beam_kernel, ch_dev, spectra_n, n_chan, batch),
+        grid=(steps,),
+        in_specs=[
+            whole((inputs, cols)),
+            whole((inputs, inputs)),
+            pl.BlockSpec((pair, double_n, inputs), lambda f: (f, 0, 0)),
+            whole((slots, beams_n)),
+        ],
+        out_specs=[
+            pl.BlockSpec((pair, 2 * spectra_n, inputs), lambda f: (f, 0, 0)),
+            pl.BlockSpec(memory_space=pl.ANY),
+        ],
+        scratch_shapes=[
+            pltpu.VMEM((inputs // 128, cols, 128), jnp.float32),
+            pltpu.VMEM(travel, jnp.bfloat16),
+            dma,
+            dma((4, n_chan)),
+            dma((4, n_chan)),
+        ],
         out_shape=[
             jax.ShapeDtypeStruct((ch_dev, 2 * spectra_n, inputs), jnp.bfloat16),
-            jax.ShapeDtypeStruct((n_chan, ch_dev, slots // n_chan, 2 * spectra_n), jnp.bfloat16),
+            jax.ShapeDtypeStruct(travel, jnp.bfloat16),
         ],
-        compiler_params=pltpu.CompilerParams(dimension_semantics=("arbitrary",)),
+        compiler_params=pltpu.CompilerParams(
+            dimension_semantics=("arbitrary",), collective_id=1, has_side_effects=True
+        ),
         name="beams",
-    )(first, gathered, perm, delays, *tables, select)
+    )(gathered, perm, weights, select)
 
 
 def visibility_kernel(sub_ref, scale_ref, left_ref, right_ref, out_ref):
@@ -442,17 +539,19 @@
         for j in range(size):
             at = (first + j) * chans
             for c in range(2):
-                out_ref[c, :, at : at + chans] = acc[
+                out_ref[:, c, at : at + chans] = acc[
                     j * count : (j + 1) * count, c * chans : (c + 1) * chans
                 ]
 
 
 def synthesize(received, taps):
-    chans, count, _ = received.shape
-    spectra_n = received.shape[2] // 2
+    n_chan, steps, count, width = received.shape
+    spectra_n = BLOCKS * SPEC
+    pair = width // (2 * spectra_n)
+    chans = n_chan * steps * pair
     frames_n = spectra_n + TAPS - 1
-    bank = received.reshape(chans, count, 2, spectra_n)
-    bank = jnp.transpose(bank, (3, 1, 2, 0)).reshape(spectra_n, count, 2 * chans)
+    bank = received.reshape(n_chan * steps, count, pair, 2, spectra_n)
+    bank = jnp.transpose(bank, (4, 1, 3, 0, 2)).reshape(spectra_n, count, 2 * chans)
     bank = jnp.pad(bank, ((TAPS - 1, TAPS - 1), (0, 0), (0, 0))).reshape(-1, 2 * chans)
     index = jnp.arange(2 * chans, dtype=jnp.int32)
     inner = index % chans
@@ -463,12 +562,11 @@
     trig = lax.optimization_barrier(trig)
     taps2 = taps.reshape(TAPS, 1, chans)
     weights = (trig[None] * jnp.concatenate([taps2, taps2], axis=2)).astype(jnp.bfloat16)
-    voices = pl.pallas_call(
+    return pl.pallas_call(
         functools.partial(voice_kernel, spectra_n, count, frames_n),
-        out_shape=jax.ShapeDtypeStruct((2, count, frames_n * chans), jnp.float32),
+        out_shape=jax.ShapeDtypeStruct((count, 2, frames_n * chans), jnp.float32),
         name="voices",
     )(bank, weights)
-    return jnp.transpose(voices, (1, 0, 2))
 
 
 def local(voltages, taps, input_id, counts, delays, beam_owner):
@@ -487,17 +585,12 @@
     position = jnp.arange(spectra_n, dtype=jnp.int32)
     valid = (position % SPEC < jnp.repeat(counts, SPEC)).astype(jnp.float32)
     total = jnp.sum(counts.astype(jnp.float32))
-    chan_index, sub_index = lax.axis_index("chan"), lax.axis_index("sub")
+    sub_index = lax.axis_index("sub")
     blocks = channelize(voltages, taps, valid, n_chan)
-    gathered = corner_turn(blocks, n_chan, n_sub).reshape(inputs, -1)
+    gathered, weights = corner_turn(blocks, delays, n_chan, n_sub)
+    gathered = gathered.reshape(inputs, -1)
     names = jnp.transpose(input_id.reshape(n_chan, n_sub, inp_dev), (1, 0, 2)).reshape(inputs)
     perm = (names[:, None] == jnp.arange(inputs, dtype=jnp.int32)[None, :]).astype(jnp.bfloat16)
-    angle = jnp.arange(chans, dtype=jnp.int32).astype(jnp.float32) * (2.0 * math.pi / chans)
-    scale = 1.0 / math.sqrt(inputs)
-    tables = [
-        (wave(angle) * scale).astype(jnp.bfloat16).astype(jnp.float32)[None, :]
-        for wave in (jnp.cos, jnp.sin)
-    ]
     owner = lax.dynamic_slice_in_dim(beam_owner[:, 0], sub_index * section, section)
     beam = jnp.arange(section, dtype=jnp.int32)
     earlier = (owner[None, :] == owner[:, None]) & (beam[None, :] < beam[:, None])
@@ -506,20 +599,9 @@
     select = (jnp.arange(n_chan * most, dtype=jnp.int32)[:, None] == target[None, :]).astype(
         jnp.bfloat16
     )
-    by_id, placed = form_beams(
-        gathered,
-        perm,
-        delays,
-        tables,
-        select,
-        (chan_index * ch_dev).astype(jnp.int32)[None],
-        ch_dev,
-        spectra_n,
-        n_chan,
-    )
-    received = lax.all_to_all(placed, "chan", split_axis=0, concat_axis=0, tiled=True)
+    by_id, received = form_beams(gathered, perm, weights, select, spectra_n, n_chan)
     visibility = correlate(by_id, (1.0 / total)[None], sub_index.astype(jnp.int32)[None], rows)
-    resynth = synthesize(received.reshape(chans, most, 2 * spectra_n), taps)
+    resynth = synthesize(received, taps)
     return (visibility, resynth)
 
 

time: 146 us -> 137 us (0.938)
  local copies, waits for them, and re-layouts: 21.6 us -> 14.3 us
  starting transfers between devices: 7.15 us -> 0 us
  Pallas kernels: 102 us -> 108 us
    all_to_all x1 -> x0, starting transfers between devices: 7.15 us -> none  [local(): lax.all_to_all(placed, 'chan', split_axis=0, concat_axis=0, tiled=True)]
    pallas_call x2, Pallas kernels: 70.6 us -> 75.7 us  [the longest x1 43 us: corner_turn(): pl.pallas_call(functools.partial(turn_kernel, n_chan, n_sub, pieces, 1.0...]
    unnamed x11, local copies, waits for them, and re-layouts: 6.83 us -> 2.79 us
    another operation x2 -> x0, local copies, waits for them, and re-layouts: 2.93 us -> none  [synthesize(): bank = received.reshape(chans, count, 2, spectra_n)]
    reshape x1 -> x2, local copies, waits for them, and re-layouts: 3.68 us -> 5.32 us  [channelize(): frames = voltages.reshape(rows, 2, frames_n, chans)]
    transpose x3 -> x1, local copies, waits for them, and re-layouts: 3.31 us -> 3.76 us  [synthesize(): jnp.transpose(bank, (4, 1, 3, 0, 2)).reshape(spectra_n, count, 2 * chans)]
  transfers between devices with their start and end apart: 1 -> 0, of which waited for: 0 -> 0; matrix products, arithmetic and copies ran while one was open for 2% -> 0% of each run, Pallas kernels for 13% -> 0%
where the time goes in v2:
time: 137 us; the launch traced here: 135 us
  Pallas kernels  108 us (79%)
  local copies, waits for them, and re-layouts  14.3 us (10%)
  other arithmetic  11.9 us (9%)
  between operations  1.45 us (1%)
    pallas_call x1, Pallas kernels, corner_turn(): pl.pallas_call(functools.partial(turn_kernel, n_chan, n_sub, pieces, 1.0...  43 us
    pallas_call x1, Pallas kernels, form_beams(): pl.pallas_call(functools.partial(beam_kernel, ch_dev, spectra_n, n_chan,...  32.6 us
    pallas_call x1, Pallas kernels, correlate(): pl.pallas_call(visibility_kernel, grid_spec=pltpu.PrefetchScalarGridSpec(...  19.7 us
    pallas_call x1, Pallas kernels, channelize(): pl.pallas_call(functools.partial(filter_kernel, rows, pairs, steps, wide,...  7.18 us
    reshape x2, local copies, waits for them, and re-layouts, channelize(): frames = voltages.reshape(rows, 2, frames_n, chans)  5.32 us
    pallas_call x1, Pallas kernels, synthesize(): pl.pallas_call(functools.partial(voice_kernel, spectra_n, count, frames_n...  5.29 us
    transpose x1, local copies, waits for them, and re-layouts, synthesize(): jnp.transpose(bank, (4, 1, 3, 0, 2)).reshape(spectra_n, count, 2 * chans)  3.76 us
    unnamed x11, local copies, waits for them, and re-layouts  2.79 us

profile of v2, /device:TPU:0, one launch (start us, length us, event | category | flops | bytes accessed | tf_op | source)
XLA Modules:
  0.0 135.4 jit_solution(1760197542355109258)
XLA Ops:
  0.6 0.0 copy-start.1
  0.6 1.3 convert_reduce_fusion.1
  2.6 3.7 %reshape.198 = bf16[64,2,43,128]{3,2,1,0:T(8,128)(2,1)S(1)} reshape(bf16[64,2,5504]{2,1,0:T(2,128)(2,1)} %param.6) | data formatting | bytes 2818048 | tf_op jit(solution)/shard_map/reshape | solution.py:150
  6.3 0.0 copy-start.3
  6.3 1.6 %copy.27 = bf16[64,2,43,128]{3,0,2,1:T(8,128)(2,1)} copy(bf16[64,2,43,128]{3,2,1,0:T(8,128)(2,1)S(1)} %reshape.198) | data formatting | bytes 2818048 | tf_op jit(solution)/shard_map/reshape | solution.py:150
  7.9 0.0 copy-done.1
  8.0 2.2 %fusion.3 = f32[256,512]{1,0:T(8,128)S(1)} fusion(s32[512]{0:T(512)S(1)} %fusion.15, s32[256]{0:T(256)S(1)} %and_select_fusion.1, pred[512]{0:T(512)(128)(4,1)S(1)} %fusion.12, pred[256]{0:T(512)(128)(4,1)S(1)} %iota_compare_fusion.3), kind=kLoop, calls=%fused_computation.13 | loop fusion | flops 2359296 | bytes 528128 | tf_op jit(solution)/shard_map/jit(_where)/select_n | solution.py:163
  10.2 2.3 %multiply_convert_fusion.w_ref = bf16[13,256,512]{2,1,0:T(8,128)(2,1)} fusion(f32[13,256]{1,0:T(8,128)S(1)} %get-tuple-element.11, f32[13,256]{1,0:T(8,128)S(1)} %get-tuple-element.10, f32[256,512]{1,0:T(8,128)S(1)} %fusion.3, pred[512]{0:T(512)(128)(4,1)S(1)} %fusion.17), kind=kLoop, calls=%fused_computation | loop fusion | flops 5111808 | bytes 3959296 | tf_op jit(solution)/shard_map/convert_element_type | solution.py:172
  12.5 0.0 copy-done.3
  12.5 0.1 broadcast_in_dim.69
  12.6 0.1 reshape.191
  12.7 0.1 slice.7
  12.8 0.1 slice.6
  12.9 0.7 broadcast_select_fusion.mask_ref
  13.6 0.0 copy-start.2
  13.6 7.2 %filterbank.1.x_ref = bf16[4,64,2048]{2,1,0:T(8,128)(2,1)} custom-call(bf16[2,43,64,128]{3,2,1,0:T(8,128)(2,1)} %bitcast.22, bf16[13,256,512]{2,1,0:T(8,128)(2,1)} %multiply_convert_fusion.w_ref, f32[16,512]{1,0:T(8,128)} %broadcast_select_fusion.mask_ref), custom_call_target="tpu_custom_call" | custom-call | tf_op jit(solution)/shard_map/filterbank/pallas_call | solution.py:174
  20.8 0.0 copy-start.4
  20.8 43.0 %corner_turn.1 = (bf16[4,4,64,2048]{3,2,1,0:T(8,128)(2,1)}, bf16[32,128,1024]{2,1,0:T(8,128)(2,1)}) custom-call(bf16[4,64,2048]{2,1,0:T(8,128)(2,1)} %filterbank.1.x_ref, s32[64,1024]{1,0:T(8,128)} %delay_ref.1), custom_call_target="tpu_custom_call" | custom-call | tf_op jit(solution)/shard_map/corner_turn/pallas_call | solution.py:336
  63.8 0.0 copy-done.2
  63.8 0.1 reshape.193
  63.9 0.1 eq.113
  64.0 1.7 %fusion.perm_ref = bf16[1024,1024]{1,0:T(8,128)(2,1)} fusion(s32[1024]{0:T(1024)S(1)} %eq.113), kind=kLoop, calls=%fused_computation.2 | loop fusion | flops 2097152 | bytes 2101248 | tf_op jit(solution)/shard_map/convert_element_type | solution.py:593
  65.7 0.0 copy-done.4
  65.7 0.1 dynamic-slice_bitcast_fusion
  65.8 0.2 convert_reduce_fusion
  66.0 0.1 multiply_add_fusion
  66.1 0.6 fusion.9.sel_ref
  66.7 32.6 %beams.1 = (bf16[32,64,1024]{2,1,0:T(8,128)(2,1)}, bf16[4,16,32,128]{3,2,1,0:T(8,128)(2,1)}) custom-call(bf16[1024,2048]{1,0:T(8,128)(2,1)} %bitcast.23, bf16[1024,1024]{1,0:T(8,128)(2,1)} %fusion.perm_ref, bf16[32,128,1024]{2,1,0:T(8,128)(2,1)} %get-tuple-element.7.weight_ref, bf16[128,64]{1,0:T(8,128)(2,1)} %fusion.9.sel_ref), custom_call_target="tpu_custom_call" | custom-call | tf_op jit(solution)/shard_map/beams/pallas_call | solution.py:455
  99.3 0.0 copy-start
  99.3 19.7 %visibility.1 = bf16[32,2,256,1024]{3,2,1,0:T(8,128)(2,1)} custom-call(s32[1]{0:T(128)} %bitcast.sub_ref, f32[1]{0:T(128)} %bitcast.1.scale_ref, bf16[32,64,1024]{2,1,0:T(8,128)(2,1)} %get-tuple-element.8.left_ref.right_ref, bf16[32,64,1024]{2,1,0:T(8,128)(2,1)} %get-tuple-element.8.left_ref.right_ref), custom_call_target="tpu_custom_call" | custom-call | flops 2147483648 | bytes 33554432 | tf_op jit(solution)/shard_map/visibility/pallas_call | solution.py:503
  119.0 0.0 copy-done
  119.0 0.8 reshape.194
  119.9 3.8 %copy.21 = bf16[32,32,2,64,2]{1,0,4,3,2:T(8,128)(2,1)} copy(bf16[32,32,2,64,2]{0,2,4,1,3:T(2,128)(2,1)S(1)} %bitcast.20) | data formatting | bytes 1048576 | tf_op jit(solution)/shard_map/transpose | solution.py:554
  123.6 2.8 %copy.25 = bf16[32,32,256]{2,1,0:T(8,128)(2,1)S(1)} copy(bf16[32,32,256]{1,0,2:T(8,128)(2,1)} %bitcast.21) | data formatting | bytes 1048576
  126.4 1.0 pad.14.clone
  127.4 1.1 fusion.7
  128.6 1.6 %multiply_convert_fusion.1.w_ref = bf16[12,256,256]{2,1,0:T(8,128)(2,1)} fusion(f32[12,256]{1,0:T(8,128)S(1)} %maximum_bitcast_fusion, f32[256,256]{1,0:T(8,128)S(1)} %fusion.7), kind=kLoop, calls=%fused_computation.3 | loop fusion | flops 1572864 | bytes 1847296 | tf_op jit(solution)/shard_map/convert_element_type | solution.py:564
  130.2 5.3 %voices.1 = f32[32,2,5504]{2,1,0:T(2,128)} custom-call(bf16[1728,256]{1,0:T(8,128)(2,1)} %bitcast.24, bf16[12,256,256]{2,1,0:T(8,128)(2,1)} %multiply_convert_fusion.1.w_ref), custom_call_target="tpu_custom_call" | custom-call | tf_op jit(solution)/shard_map/voices/pallas_call | solution.py:565
  (10 shorter events, 0.1 us)
Async XLA Ops:
  0.6 7.3 %copy-start.1 = (f32[1536]{0:T(1024)S(1)}, f32[1536]{0:T(1024)}, u32[]{:S(2)}) copy-start(f32[1536]{0:T(1024)} %param.7) | copy-start | bytes 18436
  6.3 6.2 %copy-start.3 = (s32[4]{0:T(128)S(1)}, s32[4]{0:T(128)}, u32[]{:S(2)}) copy-start(s32[4]{0:T(128)} %param.9) | copy-start | bytes 52
  13.6 50.2 %copy-start.2 = (s32[1024]{0:T(1024)S(1)}, s32[1024]{0:T(1024)}, u32[]{:S(2)}) copy-start(s32[1024]{0:T(1024)} %param.8) | copy-start | bytes 12292
  20.8 45.0 %copy-start.4 = (s32[256,1]{0,1:T(1,128)S(1)}, s32[256,1]{0,1:T(1,128)}, u32[]{:S(2)}) copy-start(s32[256,1]{0,1:T(1,128)} %param.11) | copy-start | bytes 3076
  99.3 19.7 %copy-start = (bf16[4,16,32,128]{3,2,1,0:T(8,128)(2,1)S(1)}, bf16[4,16,32,128]{3,2,1,0:T(8,128)(2,1)}, u32[]{:S(2)}) copy-start(bf16[4,16,32,128]{3,2,1,0:T(8,128)(2,1)} %get-tuple-element.9) | copy-start | bytes 1572868

commit v3 on v2

--- a/solution.py
+++ b/solution.py
@@ -178,30 +178,37 @@
     )(frames, weights, mask)
 
 
-def weigh(channel, scale, delay_ref, out_ref, f):
-    beams_n, inputs = delay_ref.shape
-    high, wide = 16, 512
-    unit = 2.0 * math.pi / NCH
+def turn_of(steps):
     quarter = NCH // 4
-
-    @pl.loop(0, beams_n // high)
-    def _(row):
-        at = pl.multiple_of(row * high, high)
-        for left in range(0, inputs, wide):
-            turn = (delay_ref[pl.ds(at, high), left : left + wide] * channel) & (NCH - 1)
-            quadrant = (turn + quarter // 2) >> (quarter.bit_length() - 1)
-            x = (turn - quadrant * quarter).astype(jnp.float32) * unit
-            y = x * x
-            even = 1.0 + y * (-1 / 2 + y * (1 / 24 + y * (-1 / 720 + y * (1 / 40320))))
-            odd = x * (1.0 + y * (-1 / 6 + y * (1 / 120 + y * (-1 / 5040 + y * (1 / 362880)))))
-            swap = (quadrant & 1) == 1
-            cosine = jnp.where(swap, odd, even) * scale
-            sine = jnp.where(swap, even, odd) * scale
-            cosine = jnp.where(((quadrant + 1) & 2) == 2, -cosine, cosine)
-            sine = jnp.where((quadrant & 2) == 2, -sine, sine)
-            out_ref[f, pl.ds(at, high), left : left + wide] = cosine.astype(jnp.bfloat16)
-            low = pl.multiple_of(at + beams_n, high)
-            out_ref[f, pl.ds(low, high), left : left + wide] = sine.astype(jnp.bfloat16)
+    turn = steps & (NCH - 1)
+    quadrant = (turn + quarter // 2) >> (quarter.bit_length() - 1)
+    x = (turn - quadrant * quarter).astype(jnp.float32) * (2.0 * math.pi / NCH)
+    y = x * x
+    even = 1.0 + y * (-1 / 2 + y * (1 / 24 + y * (-1 / 720 + y * (1 / 40320))))
+    odd = x * (1.0 + y * (-1 / 6 + y * (1 / 120 + y * (-1 / 5040 + y * (1 / 362880)))))
+    swap = (quadrant & 1) == 1
+    cosine, sine = jnp.where(swap, odd, even), jnp.where(swap, even, odd)
+    cosine = jnp.where(((quadrant + 1) & 2) == 2, -cosine, cosine)
+    return cosine, jnp.where((quadrant & 2) == 2, -sine, sine)
+
+
+def weigh(first, scale, delay_ref, out_ref, at, left, high, wide):
+    beams_n = delay_ref.shape[0]
+    delay = delay_ref[at : at + high, left : left + wide]
+    step_cos, step_sin = turn_of(delay)
+    cosine, sine = turn_of(delay * first)
+
+    def body(f, held):
+        cosine, sine = held
+        out_ref[f, at : at + high, left : left + wide] = cosine.astype(jnp.bfloat16)
+        low = at + beams_n
+        out_ref[f, low : low + high, left : left + wide] = sine.astype(jnp.bfloat16)
+        return (
+            cosine * step_cos - sine * step_sin,
+            sine * step_cos + cosine * step_sin,
+        )
+
+    lax.fori_loop(0, out_ref.shape[0], body, (cosine * scale, sine * scale))
 
 
 def turn_kernel(n_chan, n_sub, pieces, scale, x_ref, delay_ref, g_ref, weight_ref, own_sem, zs, zr, xs, xr, cs, cr):
@@ -287,18 +294,14 @@
     for h in range(pieces):
         spread(0, h)
     ch_dev = weight_ref.shape[0]
-    slots = pieces * (2 * n_chan - 1)
-    share = -(-ch_dev * 4 // (3 * slots))
-    done = [0]
+    beams_n, inputs = delay_ref.shape
+    high, wide = 16, 512
+    units = [(at, left) for at in range(0, beams_n, high) for left in range(0, inputs, wide)]
 
     def work():
-        first, last = done[0], min(ch_dev, done[0] + share)
-        done[0] = last
-        if first < last:
-
-            @pl.loop(first, last)
-            def _(f):
-                weigh(me_c * ch_dev + f, scale, delay_ref, weight_ref, f)
+        if units:
+            at, left = units.pop(0)
+            weigh(me_c * ch_dev, scale, delay_ref, weight_ref, at, left, high, wide)
 
     def relay(h):
         for j in range(n_chan):
@@ -317,7 +320,7 @@
         if h > 0:
             relay(h - 1)
     relay(pieces - 1)
-    while done[0] < ch_dev:
+    while units:
         work()
     for h in range(pieces):
         for j in range(n_chan):
@@ -329,7 +332,7 @@
 
 
 def corner_turn(blocks, delays, n_chan, n_sub):
-    pieces = 4
+    pieces = 2
     dma = pltpu.SemaphoreType.DMA
     n_x = n_sub // 2
     beams_n, inputs = delays.shape
@@ -380,13 +383,18 @@
                 (((0,), (0,)), ((), ())),
                 preferred_element_type=jnp.float32,
             )
-            for tile in range(held.shape[0]):
-                held[tile, pl.ds(at, wide), :] = sorted_part[:, tile * 128 : (tile + 1) * 128]
+            per = 2 * ch_dev
+            for q in range(wide // per):
+                to = pl.multiple_of((m * (wide // per) + q) * (per + 8), 8)
+                for tile in range(held.shape[0]):
+                    held[tile, pl.ds(to, per), :] = sorted_part[
+                        q * per : (q + 1) * per, tile * 128 : (tile + 1) * 128
+                    ]
 
         pl.semaphore_wait(barrier, n_chan - 1)
 
     def rows_of(start):
-        every = pl.ds(start, spectra_n, stride=2 * ch_dev)
+        every = pl.ds(start, spectra_n, stride=2 * ch_dev + 8)
         return jnp.concatenate([held[tile, every, :] for tile in range(held.shape[0])], axis=1)
 
     def form(j):
@@ -466,7 +474,7 @@
             pl.BlockSpec(memory_space=pl.ANY),
         ],
         scratch_shapes=[
-            pltpu.VMEM((inputs // 128, cols, 128), jnp.float32),
+            pltpu.VMEM((inputs // 128, cols + 8 * spectra_n, 128), jnp.float32),
             pltpu.VMEM(travel, jnp.bfloat16),
             dma,
             dma((4, n_chan)),

time: 137 us -> 133 us (0.971)
  Pallas kernels: 108 us -> 104 us
    pallas_call x1, Pallas kernels: 43 us -> 40.3 us  [corner_turn(): pl.pallas_call(functools.partial(turn_kernel, n_chan, n_sub, pieces, 1.0...]
where the time goes in v3:
time: 133 us; the launch traced here: 132 us
  Pallas kernels  104 us (78%)
  local copies, waits for them, and re-layouts  14.3 us (11%)
  other arithmetic  11.9 us (9%)
  between operations  1.45 us (1%)
    pallas_call x1, Pallas kernels, corner_turn(): pl.pallas_call(functools.partial(turn_kernel, n_chan, n_sub, pieces, 1.0...  40.3 us
    pallas_call x1, Pallas kernels, form_beams(): pl.pallas_call(functools.partial(beam_kernel, ch_dev, spectra_n, n_chan,...  31.8 us
    pallas_call x1, Pallas kernels, correlate(): pl.pallas_call(visibility_kernel, grid_spec=pltpu.PrefetchScalarGridSpec(...  19.5 us
    pallas_call x1, Pallas kernels, channelize(): pl.pallas_call(functools.partial(filter_kernel, rows, pairs, steps, wide,...  7.18 us
    reshape x2, local copies, waits for them, and re-layouts, channelize(): frames = voltages.reshape(rows, 2, frames_n, chans)  5.32 us
    pallas_call x1, Pallas kernels, synthesize(): pl.pallas_call(functools.partial(voice_kernel, spectra_n, count, frames_n...  5.29 us
    transpose x1, local copies, waits for them, and re-layouts, synthesize(): jnp.transpose(bank, (4, 1, 3, 0, 2)).reshape(spectra_n, count, 2 * chans)  3.76 us
    unnamed x11, local copies, waits for them, and re-layouts  2.79 us

profile of v3, /device:TPU:0, one launch (start us, length us, event | category | flops | bytes accessed | tf_op | source)
XLA Modules:
  0.0 131.7 jit_solution(11816907523933087985)
XLA Ops:
  0.6 0.0 copy-start.1
  0.6 1.3 convert_reduce_fusion.1
  2.6 3.7 %reshape.198 = bf16[64,2,43,128]{3,2,1,0:T(8,128)(2,1)S(1)} reshape(bf16[64,2,5504]{2,1,0:T(2,128)(2,1)} %param.6) | data formatting | bytes 2818048 | tf_op jit(solution)/shard_map/reshape | solution.py:150
  6.3 0.0 copy-start.3
  6.3 1.6 %copy.27 = bf16[64,2,43,128]{3,0,2,1:T(8,128)(2,1)} copy(bf16[64,2,43,128]{3,2,1,0:T(8,128)(2,1)S(1)} %reshape.198) | data formatting | bytes 2818048 | tf_op jit(solution)/shard_map/reshape | solution.py:150
  7.9 0.0 copy-done.1
  8.0 2.2 %fusion.3 = f32[256,512]{1,0:T(8,128)S(1)} fusion(s32[512]{0:T(512)S(1)} %fusion.15, s32[256]{0:T(256)S(1)} %and_select_fusion.1, pred[512]{0:T(512)(128)(4,1)S(1)} %fusion.12, pred[256]{0:T(512)(128)(4,1)S(1)} %iota_compare_fusion.3), kind=kLoop, calls=%fused_computation.13 | loop fusion | flops 2359296 | bytes 528128 | tf_op jit(solution)/shard_map/jit(_where)/select_n | solution.py:163
  10.2 2.3 %multiply_convert_fusion.w_ref = bf16[13,256,512]{2,1,0:T(8,128)(2,1)} fusion(f32[13,256]{1,0:T(8,128)S(1)} %get-tuple-element.11, f32[13,256]{1,0:T(8,128)S(1)} %get-tuple-element.10, f32[256,512]{1,0:T(8,128)S(1)} %fusion.3, pred[512]{0:T(512)(128)(4,1)S(1)} %fusion.17), kind=kLoop, calls=%fused_computation | loop fusion | flops 5111808 | bytes 3959296 | tf_op jit(solution)/shard_map/convert_element_type | solution.py:172
  12.5 0.0 copy-done.3
  12.5 0.1 broadcast_in_dim.69
  12.6 0.1 reshape.191
  12.7 0.1 slice.7
  12.8 0.1 slice.6
  12.9 0.7 broadcast_select_fusion.mask_ref
  13.6 0.0 copy-start.2
  13.6 7.2 %filterbank.1.x_ref = bf16[4,64,2048]{2,1,0:T(8,128)(2,1)} custom-call(bf16[2,43,64,128]{3,2,1,0:T(8,128)(2,1)} %bitcast.22, bf16[13,256,512]{2,1,0:T(8,128)(2,1)} %multiply_convert_fusion.w_ref, f32[16,512]{1,0:T(8,128)} %broadcast_select_fusion.mask_ref), custom_call_target="tpu_custom_call" | custom-call | tf_op jit(solution)/shard_map/filterbank/pallas_call | solution.py:174
  20.8 0.0 copy-start.4
  20.8 40.3 %corner_turn.1 = (bf16[4,4,64,2048]{3,2,1,0:T(8,128)(2,1)}, bf16[32,128,1024]{2,1,0:T(8,128)(2,1)}) custom-call(bf16[4,64,2048]{2,1,0:T(8,128)(2,1)} %filterbank.1.x_ref, s32[64,1024]{1,0:T(8,128)} %delay_ref.1), custom_call_target="tpu_custom_call" | custom-call | tf_op jit(solution)/shard_map/corner_turn/pallas_call | solution.py:339
  61.1 0.0 copy-done.2
  61.1 0.1 reshape.193
  61.2 0.1 eq.113
  61.3 1.7 %fusion.perm_ref = bf16[1024,1024]{1,0:T(8,128)(2,1)} fusion(s32[1024]{0:T(1024)S(1)} %eq.113), kind=kLoop, calls=%fused_computation.2 | loop fusion | flops 2097152 | bytes 2101248 | tf_op jit(solution)/shard_map/convert_element_type | solution.py:601
  63.0 0.0 copy-done.4
  63.0 0.1 dynamic-slice_bitcast_fusion
  63.1 0.2 convert_reduce_fusion
  63.3 0.1 multiply_add_fusion
  63.4 0.6 fusion.9.sel_ref
  64.0 31.8 %beams.1 = (bf16[32,64,1024]{2,1,0:T(8,128)(2,1)}, bf16[4,16,32,128]{3,2,1,0:T(8,128)(2,1)}) custom-call(bf16[1024,2048]{1,0:T(8,128)(2,1)} %bitcast.23, bf16[1024,1024]{1,0:T(8,128)(2,1)} %fusion.perm_ref, bf16[32,128,1024]{2,1,0:T(8,128)(2,1)} %get-tuple-element.7.weight_ref, bf16[128,64]{1,0:T(8,128)(2,1)} %fusion.9.sel_ref), custom_call_target="tpu_custom_call" | custom-call | tf_op jit(solution)/shard_map/beams/pallas_call | solution.py:463
  95.8 0.0 copy-start
  95.8 19.5 %visibility.1 = bf16[32,2,256,1024]{3,2,1,0:T(8,128)(2,1)} custom-call(s32[1]{0:T(128)} %bitcast.sub_ref, f32[1]{0:T(128)} %bitcast.1.scale_ref, bf16[32,64,1024]{2,1,0:T(8,128)(2,1)} %get-tuple-element.8.left_ref.right_ref, bf16[32,64,1024]{2,1,0:T(8,128)(2,1)} %get-tuple-element.8.left_ref.right_ref), custom_call_target="tpu_custom_call" | custom-call | flops 2147483648 | bytes 33554432 | tf_op jit(solution)/shard_map/visibility/pallas_call | solution.py:511
  115.3 0.0 copy-done
  115.3 0.8 reshape.194
  116.2 3.8 %copy.21 = bf16[32,32,2,64,2]{1,0,4,3,2:T(8,128)(2,1)} copy(bf16[32,32,2,64,2]{0,2,4,1,3:T(2,128)(2,1)S(1)} %bitcast.20) | data formatting | bytes 1048576 | tf_op jit(solution)/shard_map/transpose | solution.py:562
  119.9 2.8 %copy.25 = bf16[32,32,256]{2,1,0:T(8,128)(2,1)S(1)} copy(bf16[32,32,256]{1,0,2:T(8,128)(2,1)} %bitcast.21) | data formatting | bytes 1048576
  122.7 1.0 pad.14.clone
  123.7 1.1 fusion.7
  124.9 1.6 %multiply_convert_fusion.1.w_ref = bf16[12,256,256]{2,1,0:T(8,128)(2,1)} fusion(f32[12,256]{1,0:T(8,128)S(1)} %maximum_bitcast_fusion, f32[256,256]{1,0:T(8,128)S(1)} %fusion.7), kind=kLoop, calls=%fused_computation.3 | loop fusion | flops 1572864 | bytes 1847296 | tf_op jit(solution)/shard_map/convert_element_type | solution.py:572
  126.5 5.3 %voices.1 = f32[32,2,5504]{2,1,0:T(2,128)} custom-call(bf16[1728,256]{1,0:T(8,128)(2,1)} %bitcast.24, bf16[12,256,256]{2,1,0:T(8,128)(2,1)} %multiply_convert_fusion.1.w_ref), custom_call_target="tpu_custom_call" | custom-call | tf_op jit(solution)/shard_map/voices/pallas_call | solution.py:573
  (10 shorter events, 0.1 us)
Async XLA Ops:
  0.6 7.3 %copy-start.1 = (f32[1536]{0:T(1024)S(1)}, f32[1536]{0:T(1024)}, u32[]{:S(2)}) copy-start(f32[1536]{0:T(1024)} %param.7) | copy-start | bytes 18436
  6.3 6.2 %copy-start.3 = (s32[4]{0:T(128)S(1)}, s32[4]{0:T(128)}, u32[]{:S(2)}) copy-start(s32[4]{0:T(128)} %param.9) | copy-start | bytes 52
  13.6 47.5 %copy-start.2 = (s32[1024]{0:T(1024)S(1)}, s32[1024]{0:T(1024)}, u32[]{:S(2)}) copy-start(s32[1024]{0:T(1024)} %param.8) | copy-start | bytes 12292
  20.8 42.3 %copy-start.4 = (s32[256,1]{0,1:T(1,128)S(1)}, s32[256,1]{0,1:T(1,128)}, u32[]{:S(2)}) copy-start(s32[256,1]{0,1:T(1,128)} %param.11) | copy-start | bytes 3076
  95.8 19.5 %copy-start = (bf16[4,16,32,128]{3,2,1,0:T(8,128)(2,1)S(1)}, bf16[4,16,32,128]{3,2,1,0:T(8,128)(2,1)}, u32[]{:S(2)}) copy-start(bf16[4,16,32,128]{3,2,1,0:T(8,128)(2,1)} %get-tuple-element.9) | copy-start | bytes 1572868
